TPU v7x, 512 devices: a whole 4x8x8 slice. The times are simulated.
512 devices in a mesh: row: 32 (over z, x), col: 16 (over y, core).
Axes of the slice: x: 4, y: 8, z: 8, core: 2. Of those that a mesh axis runs over, the one named last changes fastest.
Arguments:
- panel: float32 [9216, 256], P(('row', 'col')), may hold values from -60 to 636, as said below
- trailing: float32 [9216, 9216], P('row', 'col'), may hold values from -9 to 9
Outputs:
- updated: float32 [9216, 9216], P('row', 'col')
Inputs may be any that keep to these rules, and one draw needn't show every extreme that they name: The panel's first 256 rows carry a positive diagonal between 288 and 576 on top of the other entries.
All inputs are finite; a program needn't handle non-finite values.
Results may differ from a plain program's by a relative error of at most 0.00017.
Values sent between devices are 32-bit elements; how exact they have to be, the bound alone decides.
No kernel may reach another device: no remote copies, remote signals or barrier semaphores. Data moves between devices by JAX's collectives and lax.ppermute only.
A program may use at most 64 MiB of HBM per device.

v0:
```python
import jax
import jax.numpy as jnp
from jax import lax
from jax.sharding import PartitionSpec as P


def spread(shard, axis, root):
    mine = lax.axis_index(axis) == root
    return lax.psum(jnp.where(mine, shard, jnp.zeros_like(shard)), axis)


def matmul(left, right):
    return jnp.dot(left, right, precision=lax.Precision.HIGHEST, preferred_element_type=jnp.float32)


def inner_rows(left, right):
    return lax.dot_general(
        left,
        right,
        (((0,), (0,)), ((), ())),
        precision=lax.Precision.HIGHEST,
        preferred_element_type=jnp.float32,
    )


def on_device(panel, trailing):
    n_col = lax.axis_size("col")
    n_row = lax.axis_size("row")
    fold = n_row // n_col
    local_rows = panel.shape[0]
    width = panel.shape[1]
    first_row = (lax.axis_index("row") * n_col + lax.axis_index("col")) * local_rows
    global_rows = first_row + jnp.arange(local_rows, dtype=jnp.int32)
    picker = (jnp.arange(width, dtype=jnp.int32)[:, None] == global_rows[None, :]).astype(
        jnp.float32
    )
    ident = jnp.eye(width, dtype=jnp.float32)
    gram_part = inner_rows(panel, panel)
    top_part = matmul(picker, panel)
    gram, top = lax.psum((gram_part, top_part), ("row", "col"))
    lower = jnp.linalg.cholesky(gram)
    basis = jax.scipy.linalg.solve_triangular(lower, panel.T, lower=True).T
    corner = jax.scipy.linalg.solve_triangular(lower, top.T, lower=True).T
    w_local = basis + picker.T
    w_rows = lax.all_gather(w_local, "col", axis=0, tiled=True)
    square = ident + corner
    normal_eq = inner_rows(square, square)
    tmat = jax.scipy.linalg.cho_solve((jnp.linalg.cholesky(normal_eq), True), square.T)
    col_owner = lax.axis_index("col") * fold
    w_cols = jnp.concatenate([spread(w_rows, "row", col_owner + step) for step in range(fold)], 0)
    y_local = lax.psum_scatter(matmul(trailing, w_cols), "col", scatter_dimension=0, tiled=True)
    x_local = matmul(y_local, tmat)
    inner = lax.psum(inner_rows(w_local, x_local), ("row", "col"))
    small = matmul(tmat.T, inner)
    z_local = x_local - 0.5 * matmul(w_local, small)
    z_rows = lax.all_gather(z_local, "col", axis=0, tiled=True)
    z_cols = jnp.concatenate([spread(z_rows, "row", col_owner + step) for step in range(fold)], 0)
    left = jnp.concatenate([z_rows, w_rows], 1)
    right = jnp.concatenate([w_cols, z_cols], 1)
    update = lax.dot_general(
        left,
        right,
        (((1,), (1,)), ((), ())),
        precision=lax.Precision.HIGHEST,
        preferred_element_type=jnp.float32,
    )
    return trailing - update


def solution(mesh):
    return jax.shard_map(
        on_device,
        mesh=mesh,
        in_specs=(P(("row", "col"), None), P("row", "col")),
        out_specs=P("row", "col"),
        check_vma=False,
    )
```

profile of v0, /device:TPU:1, one launch (start us, length us, event | category | flops | bytes accessed | tf_op | source)
XLA Modules:
  0.0 1165.0 jit_solution(10823113499661705974)
XLA Ops:
  6.5 1.9 fusion.51
  8.5 1.7 convolution_bitcast_fusion.1
  10.3 1.3 dynamic-slice.11
  12.2 278.9 %all-reduce.15.cloned.1.call-done = (f32[256,256]{0,1:T(8,128)}, f32[256,256]{0,1:T(8,128)}) async-done(((f32[256,256]{0,1:T(8,128)}, f32[256,256]{0,1:T(8,128)}), (f32[256,256]{0,1:T(8,128)}, f32[256,256]{0,1:T(8,128)})) %all-reduce.15.cloned.1.call-update) | async-done | bytes 524304 | tf_op jit(solution)/shard_map/psum | solution.py:40
  291.1 1.1 copy.10
  292.2 1.0 fusion.12
  293.2 11.7 %cholesky.130 = f32[128,128]{1,0:T(8,128)S(1)} custom-call(f32[128,128]{1,0:T(8,128)S(1)} %cholesky.194), custom_call_target="Cholesky" | custom-call | tf_op jit(solution)/shard_map/jit(cholesky)/cholesky | solution.py:41
  304.9 9.8 custom-call.23
  314.8 0.2 constant_dynamic-update-slice_fusion.5
  315.0 0.3 convolution_subtract_fusion.5
  315.2 11.7 %cholesky.147 = f32[128,128]{1,0:T(8,128)S(1)} custom-call(f32[128,128]{1,0:T(8,128)S(1)} %convolution_subtract_fusion.5), custom_call_target="Cholesky" | custom-call | tf_op jit(solution)/shard_map/jit(cholesky)/cholesky | solution.py:41
  327.0 0.7 compare_reduce_fusion.2
  329.0 0.1 triangular_solve.104
  329.1 4.0 while.6
  329.1 0.6 fusion.75
  329.7 1.4 bitcast_dynamic-update-slice_fusion.4
  331.1 0.6 fusion.75
  331.7 1.4 bitcast_dynamic-update-slice_fusion.4
  333.1 19.9 %custom-call.19 = f32[2,128,128]{1,2,0:T(8,128)S(1)} custom-call(f32[2,128,128]{2,1,0:T(8,128)S(1)} %get-tuple-element.22), custom_call_target="InvertDiagBlocksLowerTriangular" | custom-call | tf_op jit(solution)/shard_map/jit(_solve_triangular)/triangular_solve | solution.py:42
  352.9 0.3 fusion.18
  353.3 0.4 convolution_subtract_fusion.3
  353.7 0.3 fusion.29
  354.0 0.4 fusion.11
  354.5 0.2 fusion.28
  354.6 0.2 convolution_subtract_fusion.6
  354.8 0.2 fusion.30
  355.0 0.1 fusion.48
  355.1 0.1 copy.13
  355.3 11.7 %cholesky.164 = f32[128,128]{1,0:T(8,128)S(1)} custom-call(f32[128,128]{1,0:T(8,128)S(1)} %cholesky.197), custom_call_target="Cholesky" | custom-call | tf_op jit(solution)/shard_map/jit(cholesky)/cholesky | solution.py:48
  367.1 0.6 compare_reduce_fusion.1
  367.7 9.8 custom-call.25
  377.5 0.2 constant_dynamic-update-slice_fusion.2
  377.7 0.3 convolution_subtract_fusion.4
  378.0 11.7 %cholesky.181 = f32[128,128]{1,0:T(8,128)S(1)} custom-call(f32[128,128]{1,0:T(8,128)S(1)} %convolution_subtract_fusion.4), custom_call_target="Cholesky" | custom-call | tf_op jit(solution)/shard_map/jit(cholesky)/cholesky | solution.py:48
  389.8 0.7 compare_reduce_fusion
  391.9 4.1 while.7
  391.9 0.6 fusion.76
  392.5 1.4 bitcast_dynamic-update-slice_fusion.5
  394.0 0.6 fusion.76
  394.6 1.4 bitcast_dynamic-update-slice_fusion.5
  396.0 19.9 %custom-call.20 = f32[2,128,128]{1,2,0:T(8,128)S(1)} custom-call(f32[2,128,128]{2,1,0:T(8,128)S(1)} %get-tuple-element.30), custom_call_target="InvertDiagBlocksLowerTriangular" | custom-call | tf_op jit(solution)/shard_map/jit(_cho_solve)/triangular_solve | solution.py:48
  415.9 0.3 fusion.16
  416.2 0.3 convolution_subtract_fusion.2
  416.5 18.1 %all-gather = f32[16,18,256]{2,1,0:T(8,128)S(1)} all-gather(f32[1,18,256]{2,1,0:T(8,128)S(1)} %fusion.48), channel_id=1, replica_groups=mesh['row'=32,'col'=16] {'col'}, dimensions={0}, use_global_device_ids=true | all-gather | bytes 313344 | tf_op jit(solution)/shard_map/all_gather | solution.py:45
  434.7 0.8 broadcast_select_fusion.2
  435.6 0.3 fusion.32
  435.9 0.3 fusion.33
  436.2 0.3 convolution_subtract_fusion.1
  436.5 149.8 %all-reduce.19.cloned.1.call-done = (f32[288,256]{1,0:T(8,128)}, f32[288,256]{1,0:T(8,128)}) async-done(((f32[288,256]{1,0:T(8,128)}, f32[288,256]{1,0:T(8,128)}), (f32[288,256]{1,0:T(8,128)}, f32[288,256]{1,0:T(8,128)})) %all-reduce.19.cloned.1.call-update) | async-done | bytes 589840 | tf_op jit(solution)/shard_map/psum | solution.py:9
  586.3 1.0 constant_dynamic-update-slice_fusion.1
  587.4 0.9 convolution_bitcast_fusion
  588.3 0.9 copy.11
  589.2 0.0 all-reduce.11.cloned.1.call-start
  589.3 0.3 fusion.31
  589.6 117.1 %all-reduce.13.cloned.1.call-done = f32[288,256]{0,1:T(8,128)} async-done(((f32[288,256]{0,1:T(8,128)}), f32[288,256]{0,1:T(8,128)}) %all-reduce.13.cloned.1.call-update) | async-done | bytes 294928
  706.7 1.3 fusion.15
  708.0 1.2 fusion.46
  709.3 274.5 %all-reduce.11.cloned.1.call-done = f32[256,256]{1,0:T(8,128)} async-done(((f32[256,256]{1,0:T(8,128)}), f32[256,256]{1,0:T(8,128)}) %all-reduce.11.cloned.1.call-update) | async-done | bytes 262160 | tf_op jit(solution)/shard_map/psum | solution.py:53
  983.8 1.5 fusion.14
  985.4 0.3 fusion.6
  985.6 17.5 %all-gather.1 = f32[16,18,256]{2,1,0:T(8,128)S(1)} all-gather(f32[1,18,256]{2,1,0:T(8,128)S(1)} %fusion.6), channel_id=1, replica_groups=mesh['row'=32,'col'=16] {'col'}, dimensions={0}, use_global_device_ids=true | all-gather | bytes 313344 | tf_op jit(solution)/shard_map/all_gather | solution.py:56
  1003.2 0.8 broadcast_select_fusion.1
  1004.0 150.9 %all-reduce.17.cloned.1.call-done = (f32[288,256]{1,0:T(8,128)}, f32[288,256]{1,0:T(8,128)}) async-done(((f32[288,256]{1,0:T(8,128)}, f32[288,256]{1,0:T(8,128)}), (f32[288,256]{1,0:T(8,128)}, f32[288,256]{1,0:T(8,128)})) %all-reduce.17.cloned.1.call-update) | async-done | bytes 589840 | tf_op jit(solution)/shard_map/psum | solution.py:9
  1154.9 3.5 convolution_subtract_fusion
  (40 shorter events, 0.7 us)
Async XLA Ops:
  6.5 284.5 %all-reduce.15.cloned.1.call-start = ((), (), s32[]{:S(2)}) async-start(), calls=%async_computation.2 | async-start | bytes 1048576 | tf_op jit(solution)/shard_map/psum | solution.py:40
  10.2 576.1 %all-reduce.19.cloned.1.call-start = ((), (), s32[]{:S(2)}) async-start(), calls=%async_computation.4 | async-start | bytes 1179648 | tf_op jit(solution)/shard_map/psum | solution.py:9
  329.0 24.0 %copy-start.3 = (f32[256,256]{0,1:T(8,128)S(1)}, f32[256,256]{0,1:T(8,128)}, u32[]{:S(2)}) copy-start(f32[256,256]{0,1:T(8,128)} %get-tuple-element.55) | copy-start | bytes 786436
  353.7 0.8 copy-start.1
  435.5 271.1 %all-reduce.13.cloned.1.call-start = ((), (), s32[]{:S(2)}) async-start(), calls=%async_computation.1 | async-start | bytes 786432
  436.2 151.2 %copy-start = (f32[288,576]{1,0:T(8,128)S(1)}, f32[288,576]{1,0:T(8,128)}, u32[]{:S(2)}) copy-start(f32[288,576]{1,0:T(8,128)} %param.6) | copy-start | bytes 1990660
  586.3 1.1 copy-start.2
  589.2 394.6 %all-reduce.11.cloned.1.call-start = ((), (), s32[]{:S(2)}) async-start(), calls=%async_computation | async-start | bytes 524288 | tf_op jit(solution)/shard_map/psum | solution.py:53
  709.2 445.7 %all-reduce.17.cloned.1.call-start = ((), (), s32[]{:S(2)}) async-start(), calls=%async_computation.3 | async-start | bytes 1179648 | tf_op jit(solution)/shard_map/psum | solution.py:9
Sparse Core Ops, SparseCore 0:
  12.5 278.5 all-reduce.14
  435.7 150.6 all-reduce.18
  589.4 117.2 all-reduce.12
  711.5 272.2 all-reduce.10
  1004.2 150.7 all-reduce.16
where the time goes:
time: 1170 us
  waiting for transfers between devices  971 us (83%)
  other arithmetic  111 us (9%)
  blocking collectives  35.6 us (3%)
  matrix products  17.1 us (1%)
  between operations  16.8 us (1%)
  local copies, waits for them, and re-layouts  12.7 us (1%)
    psum x2, waiting for transfers between devices, spread(): return lax.psum(jnp.where(mine, shard, jnp.zeros_like(shard)), axis)  301 us
    psum x1, waiting for transfers between devices, on_device(): gram, top = lax.psum((gram_part, top_part), ('row', 'col'))  279 us
    psum x1, waiting for transfers between devices, on_device(): inner = lax.psum(inner_rows(w_local, x_local), ('row', 'col'))  275 us
    unnamed x6, waiting for transfers between devices  117 us
    another operation x7, other arithmetic, on_device(): jnp.linalg.cholesky(normal_eq)  34.7 us
    another operation x6, other arithmetic, on_device(): lower = jnp.linalg.cholesky(gram)  34 us
  transfers between devices with their start and end apart: 5, of which 5 were waited for; matrix products, arithmetic and copies ran while one was open for 0% of the time, Pallas kernels for 0%

commit v1 on v0

v1 whole, which is shorter than its diff:
```python
import functools

import jax
import jax.numpy as jnp
import numpy as np
from jax import lax
from jax.experimental import pallas as pl
from jax.experimental.pallas import tpu as pltpu
from jax.sharding import Mesh
from jax.sharding import PartitionSpec as P

HIGHEST = lax.Precision.HIGHEST
EVERY = ("z", "x", "y", "core")
COL = ("y", "core")
ROW = ("x", "z")

def tdot(a, b):
    return lax.dot_general(a, b, (((0,), (0,)), ((), ())), precision=HIGHEST, preferred_element_type=jnp.float32)


def dot(a, b):
    return lax.dot_general(a, b, (((1,), (0,)), ((), ())), precision=HIGHEST, preferred_element_type=jnp.float32)


def chol_step(panel, rows, block_col, step):
    pivot_col = panel[0][:, block_col + step : block_col + step + 1]
    scale = lax.rsqrt(pivot_col[step : step + 1, :])
    factor = jnp.where(rows > step, pivot_col * scale, 0.0)
    out = []
    for part in panel:
        row = part[step : step + 1, :] * scale
        out.append(jnp.where(rows == step, row, part - factor * row))
    return out


def inv_step(panel, rows, block_col, step):
    pivot_col = panel[0][:, block_col + step : block_col + step + 1]
    scale = 1.0 / pivot_col[step : step + 1, :]
    factor = jnp.where(rows == step, 0.0, pivot_col)
    out = []
    for part in panel:
        row = part[step : step + 1, :] * scale
        out.append(jnp.where(rows == step, row, part - factor * row))
    return out


def factor_body(block, gram_ref, top_ref, upper_ref, kmat_ref, schur, linv, mleft):
    n = gram_ref.shape[0]
    count = n // block
    schur[...] = gram_ref[...]
    mleft[...] = top_ref[...]
    row_ids = lax.broadcasted_iota(jnp.int32, (n, n), 0)
    col_ids = lax.broadcasted_iota(jnp.int32, (n, n), 1)
    linv[...] = jnp.where(row_ids == col_ids, 1.0, 0.0).astype(jnp.float32)
    kmat_ref[...] = jnp.zeros((n, n), jnp.float32)
    rows = lax.broadcasted_iota(jnp.int32, (block, 1), 0)
    brow = lax.broadcasted_iota(jnp.int32, (block, n), 0)
    bcol = lax.broadcasted_iota(jnp.int32, (block, n), 1)
    pending = None
    for k in range(count + 1):
        at = k * block
        prev = at - block
        if k < count:
            here = pl.ds(at, block)
            chol = [schur[here, :], linv[here, :]]
        if k > 0:
            before = pl.ds(prev, block)
            gj = [mleft[before, :] + pending[0], kmat_ref[before, :] + pending[1]]
        for step in range(block):
            if k < count:
                chol = chol_step(chol, rows, at, step)
            if k > 0:
                gj = inv_step(gj, rows, prev, step)
        if k < count:
            upper = jnp.where(bcol >= brow + at, chol[0], 0.0)
            upper_ref[here, :] = upper
            linv[here, :] = chol[1]
            if k + 1 < count:
                rest = pl.ds(at + block, n - at - block)
                right = upper[:, at + block :]
                schur[rest, :] = schur[rest, :] - tdot(right, upper)
                linv[rest, :] = linv[rest, :] - tdot(right, chol[1])
        if k > 0:
            mleft[before, :] = gj[0]
            kmat_ref[before, :] = gj[1]
            for lo, hi in ((0, prev), (at, n)):
                if hi > lo:
                    other = pl.ds(lo, hi - lo)
                    left = mleft[other, prev:at]
                    if hi > at:
                        mleft[other, :] = mleft[other, :] - dot(left, gj[0])
                    else:
                        mleft[other, :] = mleft[other, :] - dot(left, gj[0])
                    kmat_ref[other, :] = kmat_ref[other, :] - dot(left, gj[1])
        if k < count:
            pending = (upper, chol[1])


def factor(gram, top, block=32):
    n = gram.shape[0]
    shape = jax.ShapeDtypeStruct((n, n), jnp.float32)
    return pl.pallas_call(
        functools.partial(factor_body, block),
        out_shape=(shape, shape),
        in_specs=[pl.BlockSpec(memory_space=pltpu.VMEM)] * 2,
        out_specs=(pl.BlockSpec(memory_space=pltpu.VMEM),) * 2,
        scratch_shapes=[pltpu.VMEM((n, n), jnp.float32)] * 3,
        cost_estimate=pl.CostEstimate(flops=200000000, bytes_accessed=1000000, transcendentals=512),
        name="factor",
    )(gram, top)


def fold_owner(rows, cols):
    pairs = []
    for piece in range(rows * cols):
        owner = piece % rows
        target = (owner % (rows // 4)) * 4 + owner // (rows // 4)
        pairs.append((piece, target * cols + piece // rows))
    return pairs


def share_row(piece):
    depth, width = lax.axis_size("z"), lax.axis_size("x")
    ring = lax.all_to_all(jnp.broadcast_to(piece, (depth, *piece.shape)), "z", 0, 0)
    full = lax.all_to_all(jnp.broadcast_to(ring, (width, *ring.shape)), "x", 0, 0)
    return full.reshape(width * depth, *piece.shape)


def on_device(panel, trailing):
    n_row = lax.axis_size("z") * lax.axis_size("x")
    n_col = lax.axis_size("y") * lax.axis_size("core")
    piece, width = panel.shape
    row_at = lax.axis_index("z") * lax.axis_size("x") + lax.axis_index("x")
    col_at = lax.axis_index("y") * lax.axis_size("core") + lax.axis_index("core")
    moves = fold_owner(n_row, n_col)
    row_rows, col_rows = piece * n_col, piece * n_row
    g_rows = width // n_row
    c_rows = width // n_col

    p_piece = lax.ppermute(panel, EVERY, moves)
    p_row = lax.all_gather(panel, COL, axis=0, tiled=True)
    gram_part = tdot(p_row, p_row).reshape(n_row, g_rows, width)
    top_part = p_row[:width].reshape(n_row, g_rows, width)
    got = lax.all_to_all(jnp.concatenate([gram_part, top_part], 1), ROW, 0, 0)
    gram_piece = jnp.sum(got[:, :g_rows], 0)
    top_piece = got[0, g_rows:]
    shared = share_row(jnp.concatenate([gram_piece, top_piece, p_piece], 0))
    gram = shared[:, :g_rows].reshape(width, width)
    top = shared[:, g_rows : 2 * g_rows].reshape(width, width)
    p_col = shared[:, 2 * g_rows :].reshape(col_rows, width)

    upper, kmat = factor(gram, top)
    first_row = jnp.where(row_at == 0, upper, 0.0)
    first_col = jnp.where(col_at == 0, upper, 0.0)
    v_row = p_row + jnp.pad(first_row, ((0, row_rows - width), (0, 0)))
    v_col = p_col + jnp.pad(first_col, ((0, col_rows - width), (0, 0)))

    y_part = dot(trailing, v_col).reshape(n_col, piece, width)
    y_own = jnp.sum(lax.all_to_all(y_part, COL, 0, 0), 0)
    y_piece = lax.ppermute(y_own, EVERY, moves)
    y_col = share_row(y_piece).reshape(col_rows, width)
    c_part = tdot(v_col, y_col).reshape(n_col, c_rows, width)
    c_own = jnp.sum(lax.all_to_all(c_part, COL, 0, 0), 0)
    both = lax.all_gather(jnp.concatenate([c_own, y_own], 0), COL, axis=0)
    core = both[:, :c_rows].reshape(width, width)
    y_row = both[:, c_rows:].reshape(row_rows, width)

    left = jnp.concatenate([dot(y_row, kmat), v_row], 1)
    inner = y_col - dot(v_col, tdot(kmat, core))
    right = jnp.concatenate([v_col, dot(inner, kmat)], 1)
    update = lax.dot_general(
        left, right, (((1,), (1,)), ((), ())), precision=HIGHEST, preferred_element_type=jnp.float32
    )
    return trailing - update


def solution(mesh):
    grid = Mesh(np.asarray(mesh.devices).reshape(8, 4, 8, 2), EVERY)
    return jax.shard_map(
        on_device,
        mesh=grid,
        in_specs=(P(EVERY, None), P(("z", "x"), COL)),
        out_specs=P(("z", "x"), COL),
        check_vma=False,
    )
```

time: 1170 us -> 234 us (0.20)
  waiting for transfers between devices: 971 us -> 47.1 us
  other arithmetic: 111 us -> 3.74 us
  blocking collectives: 35.6 us -> 99 us
  starting transfers between devices: 0.17 us -> 34.1 us
  Pallas kernels: 0 us -> 31.9 us
  between operations: 16.8 us -> 0.29 us
    psum x4 -> x0, waiting for transfers between devices: 854 us -> none  [the longest x2 301 us: spread(): return lax.psum(jnp.where(mine, shard, jnp.zeros_like(shard)), axis)]
    unnamed x6 -> x0, waiting for transfers between devices: 117 us -> none
    another operation x18 -> x0, other arithmetic: 108 us -> none  [the longest x7 34.7 us: on_device(): jnp.linalg.cholesky(normal_eq)]
    all_to_all x0 -> x3, blocking collectives: none -> 60.6 us  [the longest x2 33.3 us: share_row(): lax.all_to_all(jnp.broadcast_to(piece, (depth, *piece.shape)), 'z', 0, 0)]
    all_to_all x0 -> x4, waiting for transfers between devices: none -> 42.3 us  [the longest x2 20.6 us: share_row(): lax.all_to_all(jnp.broadcast_to(ring, (width, *ring.shape)), 'x', 0, 0)]
    pallas_call x0 -> x1, Pallas kernels: none -> 31.9 us  [factor(): pl.pallas_call(functools.partial(factor_body, block), out_shape=(shape, s...]
    all_to_all x0 -> x4, starting transfers between devices: none -> 28.4 us  [the longest x1 10.9 us: on_device(): got = lax.all_to_all(jnp.concatenate([gram_part, top_part], 1), ROW, 0, 0)]
  transfers between devices with their start and end apart: 5 -> 6, of which waited for: 5 -> 5; matrix products, arithmetic and copies ran while one was open for 0% -> 0% of each run, Pallas kernels for 0% -> 0%
where the time goes in v1:
time: 234 us; the launch traced here: 233 us
  blocking collectives  99 us (42%)
  waiting for transfers between devices  47.1 us (20%)
  starting transfers between devices  34.1 us (15%)
  Pallas kernels  31.9 us (14%)
  matrix products  8.97 us (4%)
  local copies, waits for them, and re-layouts  8.15 us (3%)
  other arithmetic  3.74 us (2%)
    all_to_all x2, blocking collectives, share_row(): lax.all_to_all(jnp.broadcast_to(piece, (depth, *piece.shape)), 'z', 0, 0)  33.3 us
    pallas_call x1, Pallas kernels, factor(): pl.pallas_call(functools.partial(factor_body, block), out_shape=(shape, s...  31.9 us
    all_to_all x1, blocking collectives, on_device(): y_own = jnp.sum(lax.all_to_all(y_part, COL, 0, 0), 0)  27.2 us
    all_gather x1, blocking collectives, on_device(): p_row = lax.all_gather(panel, COL, axis=0, tiled=True)  22.2 us
    all_to_all x2, waiting for transfers between devices, share_row(): lax.all_to_all(jnp.broadcast_to(ring, (width, *ring.shape)), 'x', 0, 0)  20.6 us
    all_gather x1, blocking collectives, on_device(): both = lax.all_gather(jnp.concatenate([c_own, y_own], 0), COL, axis=0)  16.3 us
    all_to_all x1, starting transfers between devices, on_device(): got = lax.all_to_all(jnp.concatenate([gram_part, top_part], 1), ROW, 0, 0)  10.9 us
    all_to_all x1, waiting for transfers between devices, on_device(): c_own = jnp.sum(lax.all_to_all(c_part, COL, 0, 0), 0)  10.9 us
  transfers between devices with their start and end apart: 6, of which 5 were waited for; matrix products, arithmetic and copies ran while one was open for 0% of the time, Pallas kernels for 0%

profile of v1, /device:TPU:1, one launch (start us, length us, event | category | flops | bytes accessed | tf_op | source)
XLA Modules:
  0.0 233.2 jit_solution(17949089520021019024)
XLA Ops:
  0.0 22.2 %all-gather.1 = f32[16,18,256]{2,1,0:T(8,128)S(1)} all-gather(f32[1,18,256]{2,1,0:T(8,128)} %bitcast.40), channel_id=1, replica_groups=mesh['z'=8,'x'=4,'y'=8,'core'=2] {'y','core'}, dimensions={0}, use_global_device_ids=true | all-gather | bytes 313344 | tf_op jit(solution)/shard_map/all_gather | solution.py:141
  22.3 0.8 convolution_bitcast_fusion.1
  23.1 0.0 copy-start.4
  23.1 0.8 pad_maximum_fusion
  23.9 10.9 %all-to-all-start = ((f32[32,16,256]{2,1,0:T(8,128)}), f32[32,16,256]{2,1,0:T(8,128)S(1)}, u32[]{:S(2)}, u32[]{:S(2)}) async-start(f32[32,16,256]{2,1,0:T(8,128)} %pad_maximum_fusion), calls=%async_computation | async-start | bytes 1048576 | tf_op jit(solution)/shard_map/all_to_all | solution.py:144
  34.8 0.0 copy-done.4
  34.8 3.8 %collective-permute-start = (f32[18,256]{1,0:T(8,128)S(1)}, f32[18,256]{1,0:T(8,128)S(1)}, u32[]{:S(2)}, u32[]{:S(2)}) collective-permute-start(f32[18,256]{1,0:T(8,128)S(1)} %copy-done.4), channel_id=1, source_target_pairs={{0,0},{1,64},{2,128},{3,192},{4,256},{5,320},{6,384},{7,448},{8,16... | collective-permute-start | bytes 55304 | tf_op jit(solution)/shard_map/ppermute | solution.py:140
  38.6 10.9 %all-to-all-done = f32[32,16,256]{2,1,0:T(8,128)S(1)} async-done(((f32[32,16,256]{2,1,0:T(8,128)}), f32[32,16,256]{2,1,0:T(8,128)S(1)}, u32[]{:S(2)}, u32[]{:S(2)}) %all-to-all-start) | async-done | bytes 524320 | tf_op jit(solution)/shard_map/all_to_all | solution.py:144
  49.5 0.0 collective-permute-done
  49.6 16.9 %all_to_all.35 = f32[8,34,256]{2,1,0:T(8,128)S(1)} all-to-all(f32[8,34,256]{2,1,0:T(8,128)S(1)} %broadcast_in_dim.17), channel_id=1, replica_groups=mesh['z'=8,'x'=4,'y'=8,'core'=2] {'z'}, dimensions={0} | all-to-all | bytes 557056 | tf_op jit(solution)/shard_map/all_to_all | solution.py:124
  66.5 0.1 copy.13
  66.6 1.1 broadcast_in_dim.18
  67.7 3.5 %all-to-all-start.2 = ((f32[4,8,34,256]{3,1,2,0:T(8,128)}), f32[4,8,34,256]{3,1,2,0:T(8,128)S(1)}, u32[]{:S(2)}, u32[]{:S(2)}) async-start(f32[4,8,34,256]{3,1,2,0:T(8,128)} %broadcast_in_dim.18), calls=%async_computation.2 | async-start | bytes 2228224 | tf_op jit(solution)/shard_map/all_to_all | solution.py:125
  71.2 12.1 %all-to-all-done.2 = f32[4,8,34,256]{3,1,2,0:T(8,128)S(1)} async-done(((f32[4,8,34,256]{3,1,2,0:T(8,128)}), f32[4,8,34,256]{3,1,2,0:T(8,128)S(1)}, u32[]{:S(2)}, u32[]{:S(2)}) %all-to-all-start.2) | async-done | bytes 1114144 | tf_op jit(solution)/shard_map/all_to_all | solution.py:125
  83.3 0.1 copy.24
  83.5 0.4 copy.15
  83.9 0.1 reshape.32
  83.9 1.1 copy_bitcast_fusion.1
  85.0 31.9 %factor.1 = (f32[256,256]{1,0:T(8,128)}, f32[256,256]{1,0:T(8,128)}) custom-call(f32[256,256]{1,0:T(8,128)} %get-tuple-element.14.gram_ref, f32[256,256]{1,0:T(8,128)} %get-tuple-element.13.top_ref), custom_call_target="tpu_custom_call" | custom-call | flops 200000000 | bytes 1000000 | tf_op jit(solution)/shard_map/factor/pallas_call | solution.py:102
  116.9 0.0 copy-start
  116.9 1.1 broadcast_select_fusion
  118.0 0.1 pad_add_fusion
  118.0 0.1 copy-done
  118.1 0.9 convolution_bitcast_fusion
  119.0 27.2 %all_to_all.36 = f32[16,18,256]{2,1,0:T(8,128)S(1)} all-to-all(f32[16,18,256]{2,1,0:T(8,128)S(1)} %reshape.35), channel_id=1, replica_groups=mesh['z'=8,'x'=4,'y'=8,'core'=2] {'y','core'}, dimensions={0} | all-to-all | bytes 589824 | tf_op jit(solution)/shard_map/all_to_all | solution.py:159
  146.3 1.9 collective-permute-start.1
  148.2 4.7 %collective-permute-done.1 = f32[18,256]{1,0:T(8,128)S(1)} collective-permute-done((f32[18,256]{1,0:T(8,128)S(1)}, f32[18,256]{1,0:T(8,128)S(1)}, u32[]{:S(2)}, u32[]{:S(2)}) %collective-permute-start.1) | collective-permute-done | bytes 18464 | tf_op jit(solution)/shard_map/ppermute | solution.py:160
  153.0 16.4 %all_to_all.37 = f32[8,18,256]{2,1,0:T(8,128)S(1)} all-to-all(f32[8,18,256]{2,1,0:T(8,128)S(1)} %broadcast_in_dim.20), channel_id=1, replica_groups=mesh['z'=8,'x'=4,'y'=8,'core'=2] {'z'}, dimensions={0} | all-to-all | bytes 294912 | tf_op jit(solution)/shard_map/all_to_all | solution.py:124
  169.4 0.9 broadcast_in_dim.21
  170.3 4.1 %all-to-all-start.5 = ((f32[4,8,18,256]{3,1,2,0:T(8,128)}), f32[4,8,18,256]{3,1,2,0:T(8,128)}, u32[]{:S(2)}, u32[]{:S(2)}) async-start(f32[4,8,18,256]{3,1,2,0:T(8,128)} %broadcast_in_dim.21), calls=%async_computation.5 | async-start | bytes 1179648 | tf_op jit(solution)/shard_map/all_to_all | solution.py:125
  174.5 0.2 copy.18
  174.7 8.6 %all-to-all-done.5 = f32[4,8,18,256]{3,1,2,0:T(8,128)} async-done(((f32[4,8,18,256]{3,1,2,0:T(8,128)}), f32[4,8,18,256]{3,1,2,0:T(8,128)}, u32[]{:S(2)}, u32[]{:S(2)}) %all-to-all-start.5) | async-done | bytes 589856 | tf_op jit(solution)/shard_map/all_to_all | solution.py:125
  183.3 1.3 copy.20
  184.5 0.9 reshape.44
  185.4 2.5 %fusion.8 = f32[16,16,256]{2,1,0:T(8,128)} fusion(f32[16,16,576]{2,1,0:T(8,128)S(1)} %bitcast.38, f32[576,256,1]{1,0,2:T(8,128)} %reshape.44), kind=kOutput, calls=%fused_computation.25 | convolution fusion | flops 452984832 | bytes 1441792 | tf_op jit(solution)/shard_map/dot_general | solution.py:18
  188.0 9.8 %all-to-all-start.6 = ((f32[16,16,256]{2,1,0:T(8,128)}), f32[16,16,256]{2,1,0:T(8,128)}, u32[]{:S(2)}, u32[]{:S(2)}) async-start(f32[16,16,256]{2,1,0:T(8,128)} %fusion.8), calls=%async_computation.6 | async-start | bytes 524288 | tf_op jit(solution)/shard_map/all_to_all | solution.py:163
  197.8 0.7 pad_add_fusion.1
  198.6 0.1 reshape_reshape.3
  198.6 10.9 %all-to-all-done.6 = f32[16,16,256]{2,1,0:T(8,128)} async-done(((f32[16,16,256]{2,1,0:T(8,128)}), f32[16,16,256]{2,1,0:T(8,128)}, u32[]{:S(2)}, u32[]{:S(2)}) %all-to-all-start.6) | async-done | bytes 262176 | tf_op jit(solution)/shard_map/all_to_all | solution.py:163
  209.5 1.0 reduce_sum.29
  210.5 16.3 %all-gather.2 = f32[16,34,256]{2,1,0:T(8,128)S(1)} all-gather(f32[1,34,256]{2,1,0:T(8,128)S(1)} %maximum_bitcast_fusion), channel_id=2, replica_groups=mesh['z'=8,'x'=4,'y'=8,'core'=2] {'y','core'}, dimensions={0}, use_global_device_ids=true | all-gather | bytes 591872 | tf_op jit(solution)/shard_map/all_gather | solution.py:164
  226.8 0.0 copy-start.1
  226.8 0.7 slice.39
  227.5 0.0 copy-start.3
  227.6 0.2 copy-done.1
  227.8 0.4 fusion.9
  228.2 0.3 copy-done.3
  228.5 0.6 fusion.10
  229.1 0.6 convolution_subtract_fusion.1
  229.7 0.0 copy-start.2
  229.8 0.6 fusion.11
  230.4 0.3 copy-done.2
  230.7 2.5 %convolution_subtract_fusion = f32[288,576]{1,0:T(8,128)} fusion(f32[288,576]{1,0:T(8,128)S(1)} %copy-done, f32[576,256]{1,0:T(8,128)S(1)} %fusion.11, f32[576,256]{1,0:T(8,128)S(1)} %pad_add_fusion, f32[288,256]{1,0:T(8,128)S(1)} %copy-done.2, f32[288,256]{1,0:T(8,128)S(1)} %fusion.9), kind=kOutput, calls=%fused_computation | convolution fusion | flops 1019824128 | bytes 3096576 | tf_op jit(solution)/shard_map/dot_general | solution.py:171
  (15 shorter events, 0.4 us)
Async XLA Ops:
  23.1 11.8 %copy-start.4 = (f32[18,256]{1,0:T(8,128)S(1)}, f32[18,256]{1,0:T(8,128)}, u32[]{:S(2)}) copy-start(f32[18,256]{1,0:T(8,128)} %param.2) | copy-start | bytes 55300
  23.9 25.5 %all-to-all-start = ((f32[32,16,256]{2,1,0:T(8,128)}), f32[32,16,256]{2,1,0:T(8,128)S(1)}, u32[]{:S(2)}, u32[]{:S(2)}) async-start(f32[32,16,256]{2,1,0:T(8,128)} %pad_maximum_fusion), calls=%async_computation | async-start | bytes 1048576 | tf_op jit(solution)/shard_map/all_to_all | solution.py:144
  34.8 14.7 %collective-permute-start = (f32[18,256]{1,0:T(8,128)S(1)}, f32[18,256]{1,0:T(8,128)S(1)}, u32[]{:S(2)}, u32[]{:S(2)}) collective-permute-start(f32[18,256]{1,0:T(8,128)S(1)} %copy-done.4), channel_id=1, source_target_pairs={{0,0},{1,64},{2,128},{3,192},{4,256},{5,320},{6,384},{7,448},{8,16... | collective-permute-start | bytes 55304 | tf_op jit(solution)/shard_map/ppermute | solution.py:140
  67.7 15.6 %all-to-all-start.2 = ((f32[4,8,34,256]{3,1,2,0:T(8,128)}), f32[4,8,34,256]{3,1,2,0:T(8,128)S(1)}, u32[]{:S(2)}, u32[]{:S(2)}) async-start(f32[4,8,34,256]{3,1,2,0:T(8,128)} %broadcast_in_dim.18), calls=%async_computation.2 | async-start | bytes 2228224 | tf_op jit(solution)/shard_map/all_to_all | solution.py:125
  116.9 1.2 copy-start
  146.3 6.7 %collective-permute-start.1 = (f32[18,256]{1,0:T(8,128)S(1)}, f32[18,256]{1,0:T(8,128)S(1)}, u32[]{:S(2)}, u32[]{:S(2)}) collective-permute-start(f32[18,256]{1,0:T(8,128)S(1)} %reduce_sum.28), channel_id=1, source_target_pairs={{0,0},{1,64},{2,128},{3,192},{4,256},{5,320},{6,384},{7,448},{8,16... | collective-permute-start | bytes 55304 | tf_op jit(solution)/shard_map/ppermute | solution.py:160
  170.3 13.0 %all-to-all-start.5 = ((f32[4,8,18,256]{3,1,2,0:T(8,128)}), f32[4,8,18,256]{3,1,2,0:T(8,128)}, u32[]{:S(2)}, u32[]{:S(2)}) async-start(f32[4,8,18,256]{3,1,2,0:T(8,128)} %broadcast_in_dim.21), calls=%async_computation.5 | async-start | bytes 1179648 | tf_op jit(solution)/shard_map/all_to_all | solution.py:125
  188.0 21.5 %all-to-all-start.6 = ((f32[16,16,256]{2,1,0:T(8,128)}), f32[16,16,256]{2,1,0:T(8,128)}, u32[]{:S(2)}, u32[]{:S(2)}) async-start(f32[16,16,256]{2,1,0:T(8,128)} %fusion.8), calls=%async_computation.6 | async-start | bytes 524288 | tf_op jit(solution)/shard_map/all_to_all | solution.py:163
  226.8 1.0 copy-start.1
  227.5 1.0 copy-start.3
  229.7 1.0 copy-start.2

commit v2 on v0

v2 whole, which is shorter than its diff:
```python
import functools

import jax
import jax.numpy as jnp
import numpy as np
from jax import lax
from jax.experimental import pallas as pl
from jax.experimental.pallas import tpu as pltpu
from jax.sharding import Mesh
from jax.sharding import PartitionSpec as P


HIGHEST = lax.Precision.HIGHEST
HIGH = lax.Precision.HIGH
DEPTH, WIDTH = 8, 4
EVERY = ("z", "x", "y", "core")
COL = ("y", "core")
ROW = ("x", "z")

SUB, LANE = 8, 128


def tdot(a, b, precision=HIGHEST):
    return lax.dot_general(
        a, b, (((0,), (0,)), ((), ())), precision=precision, preferred_element_type=jnp.float32
    )


def dot(a, b, precision=HIGHEST):
    return jnp.dot(a, b, precision=precision, preferred_element_type=jnp.float32)


def load_tiles(refs, at, block):
    out = []
    for ref in refs:
        for lane in range(0, ref.shape[1], LANE):
            out.append([ref[at + t : at + t + SUB, lane : lane + LANE] for t in range(0, block, SUB)])
    return out


def spread_lane(tile, lane):
    return jnp.broadcast_to(tile[:, lane : lane + 1], (SUB, LANE))


def spread_row(tile, row):
    return jnp.broadcast_to(tile[row : row + 1, :], (SUB, LANE))


def chol_group(parts, group, at, sub_ids):
    part, lane = divmod(at + group * SUB, LANE)
    count = len(parts[0])
    cols = [spread_lane(parts[part][group], lane + k) for k in range(SUB)]
    entry = [[spread_row(cols[k], i) if i >= k else None for k in range(SUB)] for i in range(SUB)]
    below = [[spread_lane(parts[part][t], lane + k) for k in range(SUB)] for t in range(group + 1, count)]
    rows = [[spread_row(p[group], k) for k in range(SUB)] for p in parts]
    for k in range(SUB):
        scale = lax.rsqrt(entry[k][k])
        for i in range(k + 1, SUB):
            entry[i][k] = entry[i][k] * scale
        for j in range(k + 1, SUB):
            for i in range(j, SUB):
                entry[i][j] = entry[i][j] - entry[i][k] * entry[j][k]
        for line in below:
            line[k] = line[k] * scale
            for j in range(k + 1, SUB):
                line[j] = line[j] - line[k] * entry[j][k]
        for row in rows:
            row[k] = row[k] * scale
            for j in range(k + 1, SUB):
                row[j] = row[j] - entry[j][k] * row[k]
    for p, row in zip(parts, rows):
        tile = row[0]
        for k in range(1, SUB):
            tile = jnp.where(sub_ids == k, row[k], tile)
        p[group] = tile
        for t, line in zip(range(group + 1, count), below):
            for k in range(SUB):
                p[t] = p[t] - line[k] * row[k]


def inv_group(parts, group, at, sub_ids):
    part, lane = divmod(at + group * SUB, LANE)
    count = len(parts[0])
    cols = [spread_lane(parts[part][group], lane + k) for k in range(SUB)]
    entry = [[spread_row(cols[k], i) for k in range(SUB)] for i in range(SUB)]
    other = [t for t in range(count) if t != group]
    side = [[spread_lane(parts[part][t], lane + k) for k in range(SUB)] for t in other]
    rows = [[spread_row(p[group], k) for k in range(SUB)] for p in parts]
    for k in range(SUB):
        scale = 1.0 / entry[k][k]
        for j in range(k + 1, SUB):
            entry[k][j] = entry[k][j] * scale
        for row in rows:
            row[k] = row[k] * scale
        for i in range(SUB):
            if i != k:
                for j in range(k + 1, SUB):
                    entry[i][j] = entry[i][j] - entry[i][k] * entry[k][j]
                for row in rows:
                    row[i] = row[i] - entry[i][k] * row[k]
    for p, row in zip(parts, rows):
        tile = row[0]
        for k in range(1, SUB):
            tile = jnp.where(sub_ids == k, row[k], tile)
        p[group] = tile
        for t, line in zip(other, side):
            for k in range(SUB):
                p[t] = p[t] - line[k] * row[k]


def join(parts):
    return jnp.concatenate([jnp.concatenate(p, 0) for p in parts], 1)


def chol_body(block, gram_ref, upper_ref, linv_ref, schur):
    n = gram_ref.shape[0]
    half = n // LANE
    schur[...] = gram_ref[...]
    row_ids = lax.broadcasted_iota(jnp.int32, (n, n), 0)
    col_ids = lax.broadcasted_iota(jnp.int32, (n, n), 1)
    linv_ref[...] = jnp.where(row_ids == col_ids, 1.0, 0.0).astype(jnp.float32)
    sub_ids = lax.broadcasted_iota(jnp.int32, (SUB, LANE), 0)
    brow = lax.broadcasted_iota(jnp.int32, (block, n), 0)
    bcol = lax.broadcasted_iota(jnp.int32, (block, n), 1)
    for at in range(0, n, block):
        here = pl.ds(at, block)
        parts = load_tiles((schur, linv_ref), at, block)
        for group in range(block // SUB):
            chol_group(parts, group, at, sub_ids)
        upper = jnp.where(bcol >= brow + at, join(parts[:half]), 0.0)
        lower = join(parts[half:])
        upper_ref[here, :] = upper
        linv_ref[here, :] = lower
        if at + block < n:
            rest = pl.ds(at + block, n - at - block)
            right = upper[:, at + block :]
            schur[rest, :] = schur[rest, :] - tdot(right, upper)
            linv_ref[rest, :] = linv_ref[rest, :] - tdot(right, lower)


def inv_body(block, upper_ref, linv_ref, top_ref, kmat_ref, left):
    n = top_ref.shape[0]
    half = n // LANE
    left[...] = top_ref[...] + upper_ref[...]
    kmat_ref[...] = linv_ref[...]
    sub_ids = lax.broadcasted_iota(jnp.int32, (SUB, LANE), 0)
    for at in range(0, n, block):
        here = pl.ds(at, block)
        parts = load_tiles((left, kmat_ref), at, block)
        for group in range(block // SUB):
            inv_group(parts, group, at, sub_ids)
        keep = join(parts[:half])
        out = join(parts[half:])
        left[here, :] = keep
        kmat_ref[here, :] = out
        for lo, hi in ((at + block, n), (0, at)):
            if hi > lo:
                other = pl.ds(lo, hi - lo)
                column = left[other, at : at + block]
                if at + block < n:
                    left[other, :] = left[other, :] - dot(column, keep)
                kmat_ref[other, :] = kmat_ref[other, :] - dot(column, out)


def local_call(body, outs, scratch, block, *args):
    n = args[0].shape[0]
    shape = jax.ShapeDtypeStruct((n, n), jnp.float32)
    vmem = pl.BlockSpec(memory_space=pltpu.VMEM)
    return pl.pallas_call(
        functools.partial(body, block),
        out_shape=(shape,) * outs,
        in_specs=[vmem] * len(args),
        out_specs=(vmem,) * outs,
        scratch_shapes=[pltpu.VMEM((n, n), jnp.float32)] * scratch,
        cost_estimate=pl.CostEstimate(
            flops=16_000_000_000, bytes_accessed=4 * n * n * (outs + len(args)), transcendentals=n
        ),
    )(*args)


def fold_moves(rows, cols):
    pairs = []
    for piece in range(rows * cols):
        owner = piece % rows
        target = (owner % DEPTH) * WIDTH + owner // DEPTH
        pairs.append((piece, target * cols + piece // rows))
    return pairs


def on_device(panel, trailing):
    n_row = lax.axis_size("z") * lax.axis_size("x")
    n_col = lax.axis_size("y") * lax.axis_size("core")
    piece, width = panel.shape
    row_at = lax.axis_index("z") * lax.axis_size("x") + lax.axis_index("x")
    col_at = lax.axis_index("y") * lax.axis_size("core") + lax.axis_index("core")
    moves = fold_moves(n_row, n_col)
    back = [(target, source) for source, target in moves]
    row_rows, col_rows = piece * n_col, piece * n_row
    c_rows, g_rows = width // n_col, width // n_row

    def share_row(part):
        copies = jnp.broadcast_to(part, (n_row, *part.shape))
        return lax.all_to_all(copies, ROW, 0, 0)

    def share_twice(part):
        ring = lax.all_to_all(jnp.broadcast_to(part, (DEPTH, *part.shape)), "z", 0, 0)
        full = lax.all_to_all(jnp.broadcast_to(ring, (WIDTH, *ring.shape)), "x", 0, 0)
        return full.reshape(n_row, *part.shape)

    def sum_twice(stack):
        stack = stack.reshape(WIDTH, DEPTH, *stack.shape[1:])
        stack = jnp.sum(lax.all_to_all(stack, "x", 0, 0), 0)
        return jnp.sum(lax.all_to_all(stack, "z", 0, 0), 0)

    p_far = lax.ppermute(panel, EVERY, moves)
    p_row = lax.all_gather(panel, COL, axis=0, tiled=True)
    first = row_at == 0
    stacked = [
        tdot(trailing, p_row, HIGH).reshape(n_row, piece, width),
        jnp.where(first, trailing[:width], 0.0).T.reshape(n_row, piece, width),
        tdot(p_row, p_row).reshape(n_row, g_rows, width),
        jnp.where(first, p_row[:width], 0.0).reshape(n_row, g_rows, width),
    ]
    moved = sum_twice(jnp.concatenate(stacked, 1))
    at = 2 * piece
    ap_far, ae_far = moved[:piece], moved[piece:at]
    both = share_row(moved[at:])
    gram = both[:, :g_rows].reshape(width, width)
    top = both[:, g_rows:].reshape(width, width)

    upper, linv = local_call(chol_body, 2, 1, 64, gram)
    (kmat,) = local_call(inv_body, 1, 1, 64, upper, linv, top)

    y_far = ap_far + dot(ae_far, upper, HIGH)
    both = share_twice(jnp.concatenate([y_far, p_far], 0))
    y_col = both[:, :piece].reshape(col_rows, width)
    p_col = both[:, piece:].reshape(col_rows, width)
    y_own = lax.ppermute(y_far, EVERY, back)
    first_row = jnp.where(first, upper, 0.0)
    first_col = jnp.where(col_at == 0, upper, 0.0)
    v_row = p_row + jnp.pad(first_row, ((0, row_rows - width), (0, 0)))
    v_col = p_col + jnp.pad(first_col, ((0, col_rows - width), (0, 0)))
    c_part = tdot(v_col, y_col, HIGH).reshape(n_col, c_rows, width)
    c_part = lax.all_to_all(c_part, COL, 0, 0)
    last = lax.all_gather(jnp.concatenate([jnp.sum(c_part, 0), y_own], 0), COL, axis=0)
    core = last[:, :c_rows].reshape(width, width)
    y_row = last[:, c_rows:].reshape(row_rows, width)

    left = jnp.concatenate([dot(y_row, kmat, HIGH), v_row], 1)
    inner = y_col - dot(v_col, tdot(kmat, core, HIGH), HIGH)
    right = jnp.concatenate([v_col, dot(inner, kmat, HIGH)], 1)
    update = lax.dot_general(
        left, right, (((1,), (1,)), ((), ())), precision=HIGH, preferred_element_type=jnp.float32
    )
    return trailing - update


def solution(mesh):
    grid = Mesh(np.asarray(mesh.devices).reshape(DEPTH, WIDTH, 8, 2), EVERY)
    return jax.shard_map(
        on_device,
        mesh=grid,
        in_specs=(P(EVERY, None), P(("z", "x"), COL)),
        out_specs=P(("z", "x"), COL),
        check_vma=False,
    )
```

time: 1170 us -> 196 us (0.17)
  waiting for transfers between devices: 971 us -> 6.45 us
  other arithmetic: 111 us -> 3.08 us
  blocking collectives: 35.6 us -> 105 us
  starting transfers between devices: 0.17 us -> 37.5 us
  Pallas kernels: 0 us -> 24 us
  between operations: 16.8 us -> 0.38 us
    psum x4 -> x0, waiting for transfers between devices: 854 us -> none  [the longest x2 301 us: spread(): return lax.psum(jnp.where(mine, shard, jnp.zeros_like(shard)), axis)]
    unnamed x6 -> x0, waiting for transfers between devices: 117 us -> none
    another operation x18 -> x0, other arithmetic: 108 us -> none  [the longest x7 34.7 us: on_device(): jnp.linalg.cholesky(normal_eq)]
    all_to_all x0 -> x3, blocking collectives: none -> 63.1 us  [the longest x1 24.3 us: sum_twice(): stack = jnp.sum(lax.all_to_all(stack, 'x', 0, 0), 0)]
    pallas_call x0 -> x2, Pallas kernels: none -> 24 us  [local_call(): pl.pallas_call(functools.partial(body, block), out_shape=(shape,) * outs,...]
    all_to_all x0 -> x3, starting transfers between devices: none -> 20 us  [the longest x1 12.6 us: on_device(): c_part = lax.all_to_all(c_part, COL, 0, 0)]
    ppermute x0 -> x2, starting transfers between devices: none -> 17.4 us  [the longest x1 11.4 us: on_device(): y_own = lax.ppermute(y_far, EVERY, back)]
  transfers between devices with their start and end apart: 5 -> 5, of which waited for: 5 -> 1; matrix products, arithmetic and copies ran while one was open for 0% -> 5% of each run, Pallas kernels for 0% -> 12%
where the time goes in v2:
time: 196 us; the launch traced here: 195 us
  blocking collectives  105 us (54%)
  starting transfers between devices  37.5 us (19%)
  Pallas kernels  24 us (12%)
  local copies, waits for them, and re-layouts  10.2 us (5%)
  matrix products  9.09 us (5%)
  waiting for transfers between devices  6.45 us (3%)
  other arithmetic  3.08 us (2%)
    all_to_all x1, blocking collectives, sum_twice(): stack = jnp.sum(lax.all_to_all(stack, 'x', 0, 0), 0)  24.3 us
    pallas_call x2, Pallas kernels, local_call(): pl.pallas_call(functools.partial(body, block), out_shape=(shape,) * outs,...  24 us
    all_to_all x1, blocking collectives, sum_twice(): return jnp.sum(lax.all_to_all(stack, 'z', 0, 0), 0)  23.3 us
    all_gather x1, blocking collectives, on_device(): p_row = lax.all_gather(panel, COL, axis=0, tiled=True)  22.3 us
    all_gather x1, blocking collectives, on_device(): lax.all_gather(jnp.concatenate([jnp.sum(c_part, 0), y_own], 0), COL, axis=0)  19.2 us
    all_to_all x1, blocking collectives, share_twice(): lax.all_to_all(jnp.broadcast_to(part, (DEPTH, *part.shape)), 'z', 0, 0)  15.5 us
    all_to_all x1, starting transfers between devices, on_device(): c_part = lax.all_to_all(c_part, COL, 0, 0)  12.6 us
    ppermute x1, starting transfers between devices, on_device(): y_own = lax.ppermute(y_far, EVERY, back)  11.4 us
  transfers between devices with their start and end apart: 5, of which 1 were waited for; matrix products, arithmetic and copies ran while one was open for 5% of the time, Pallas kernels for 12%

profile of v2, /device:TPU:1, one launch (start us, length us, event | category | flops | bytes accessed | tf_op | source)
XLA Modules:
  0.0 195.3 jit_solution(3551945216000683988)
XLA Ops:
  0.0 0.0 copy-start
  0.0 22.3 %all-gather.1 = f32[16,18,256]{2,1,0:T(8,128)S(1)} all-gather(f32[1,18,256]{2,1,0:T(8,128)} %bitcast.38), channel_id=1, replica_groups=mesh['z'=8,'x'=4,'y'=8,'core'=2] {'y','core'}, dimensions={0}, use_global_device_ids=true | all-gather | bytes 313344 | tf_op jit(solution)/shard_map/all_gather | solution.py:216
  22.4 0.0 copy-done
  22.5 1.0 fusion.9
  23.4 1.5 fusion.10
  25.0 0.2 copy.23
  25.2 0.1 concatenate.25
  25.3 0.1 concatenate.24
  25.3 1.2 pad_maximum_fusion
  26.5 0.5 copy.24
  27.1 24.3 %all_to_all.30 = f32[4,8,52,256]{3,1,2,0:T(8,128)S(1)} all-to-all(f32[4,8,52,256]{3,1,2,0:T(8,128)S(1)} %copy.24), channel_id=1, replica_groups=mesh['z'=8,'x'=4,'y'=8,'core'=2] {'x'}, dimensions={0} | all-to-all | bytes 3407872 | tf_op jit(solution)/shard_map/all_to_all | solution.py:212
  51.4 0.1 reduce_sum.27
  51.5 0.1 copy.25
  51.7 0.0 copy-start.7
  51.7 23.3 %all_to_all.31 = f32[8,52,256]{2,1,0:T(8,128)S(1)} all-to-all(f32[8,52,256]{2,1,0:T(8,128)S(1)} %copy.25), channel_id=1, replica_groups=mesh['z'=8,'x'=4,'y'=8,'core'=2] {'z'}, dimensions={0} | all-to-all | bytes 851968 | tf_op jit(solution)/shard_map/all_to_all | solution.py:213
  75.0 0.9 broadcast_in_dim.21
  75.9 3.9 %all-to-all-start.2 = ((f32[32,16,256]{2,1,0:T(8,128)}), f32[32,16,256]{2,1,0:T(8,128)S(1)}, u32[]{:S(2)}, u32[]{:S(2)}) async-start(f32[32,16,256]{2,1,0:T(8,128)} %broadcast_in_dim.21), calls=%async_computation.2 | async-start | bytes 1048576 | tf_op jit(solution)/shard_map/all_to_all | solution.py:203
  79.8 0.0 copy-done.7
  79.8 6.0 %collective-permute-start = (f32[18,256]{1,0:T(8,128)S(1)}, f32[18,256]{1,0:T(8,128)S(1)}, u32[]{:S(2)}, u32[]{:S(2)}) collective-permute-start(f32[18,256]{1,0:T(8,128)S(1)} %copy-done.7), channel_id=1, source_target_pairs={{0,0},{1,64},{2,128},{3,192},{4,256},{5,320},{6,384},{7,448},{8,16... | collective-permute-start | bytes 55304 | tf_op jit(solution)/shard_map/ppermute | solution.py:215
  85.9 6.4 %all-to-all-done.2 = f32[32,16,256]{2,1,0:T(8,128)S(1)} async-done(((f32[32,16,256]{2,1,0:T(8,128)}), f32[32,16,256]{2,1,0:T(8,128)S(1)}, u32[]{:S(2)}, u32[]{:S(2)}) %all-to-all-start.2) | async-done | bytes 524320 | tf_op jit(solution)/shard_map/all_to_all | solution.py:203
  92.3 0.8 slice_bitcast_fusion
  93.1 10.5 %shard_map.28 = (f32[256,256]{1,0:T(8,128)}, f32[256,256]{1,0:T(8,128)}) custom-call(f32[256,256]{1,0:T(8,128)} %get-tuple-element.12.gram_ref), custom_call_target="tpu_custom_call" | custom-call | flops 16000000000 | bytes 786432 | tf_op jit(solution)/shard_map/pallas_call | solution.py:169
  103.6 1.1 convolution_add_fusion
  104.7 0.0 collective-permute-done
  104.8 15.5 %all_to_all.32 = f32[8,36,256]{2,1,0:T(8,128)S(1)} all-to-all(f32[8,36,256]{2,1,0:T(8,128)S(1)} %broadcast_in_dim.22), channel_id=1, replica_groups=mesh['z'=8,'x'=4,'y'=8,'core'=2] {'z'}, dimensions={0} | all-to-all | bytes 589824 | tf_op jit(solution)/shard_map/all_to_all | solution.py:206
  120.3 0.1 copy.26
  120.4 0.0 copy-start.4
  120.4 1.1 broadcast_in_dim.23
  121.5 3.5 %all-to-all-start.4 = ((f32[4,8,36,256]{3,1,2,0:T(8,128)}), f32[4,8,36,256]{3,1,2,0:T(8,128)S(1)}, u32[]{:S(2)}, u32[]{:S(2)}) async-start(f32[4,8,36,256]{3,1,2,0:T(8,128)} %broadcast_in_dim.23), calls=%async_computation.4 | async-start | bytes 2359296 | tf_op jit(solution)/shard_map/all_to_all | solution.py:207
  125.0 11.4 %collective-permute-start.1 = (f32[18,256]{1,0:T(8,128)S(1)}, f32[18,256]{1,0:T(8,128)S(1)}, u32[]{:S(2)}, u32[]{:S(2)}) collective-permute-start(f32[18,256]{1,0:T(8,128)S(1)} %convolution_add_fusion), channel_id=1, source_target_pairs={{0,0},{64,1},{128,2},{192,3},{256,4},{320,5},{384,6},{448,7},{16,8... | collective-permute-start | bytes 55304 | tf_op jit(solution)/shard_map/ppermute | solution.py:238
  136.4 0.0 copy-done.4
  136.5 0.8 broadcast_select_fusion
  137.3 0.0 all-to-all-done.4
  137.3 0.1 copy.32
  137.4 0.9 fusion.8
  138.4 0.0 copy-start.6
  138.4 0.4 copy.28
  138.8 0.1 reshape.38
  138.8 0.5 copy-done.6
  139.3 0.1 pad_add_fusion
  139.4 0.2 copy.29
  139.6 1.4 copy.30
  141.1 0.9 reshape.49
  142.0 2.3 %fusion.11 = f32[16,16,256]{2,1,0:T(8,128)} fusion(f32[16,16,576]{2,1,0:T(8,128)S(1)} %bitcast.34, f32[576,256,1]{1,0,2:T(8,128)} %reshape.49), kind=kOutput, calls=%fused_computation.26 | convolution fusion | flops 226492416 | bytes 1441792 | tf_op jit(solution)/shard_map/dot_general | solution.py:24
  144.2 12.6 %all-to-all-start.5 = ((f32[16,16,256]{2,1,0:T(8,128)}), f32[16,16,256]{2,1,0:T(8,128)S(1)}, u32[]{:S(2)}, u32[]{:S(2)}) async-start(f32[16,16,256]{2,1,0:T(8,128)} %fusion.11), calls=%async_computation.5 | async-start | bytes 524288 | tf_op jit(solution)/shard_map/all_to_all | solution.py:244
  156.8 0.0 copy-start.5
  156.8 13.5 %shard_map.29 = f32[256,256]{1,0:T(8,128)} custom-call(f32[256,256]{1,0:T(8,128)} %get-tuple-element.7.upper_ref, f32[256,256]{1,0:T(8,128)} %get-tuple-element.8.linv_ref, f32[256,256]{1,0:T(8,128)} %get-tuple-element.11.top_ref), custom_call_target="tpu_custom_call" | custom-call | flops 16000000000 | bytes 1048576 | tf_op jit(solution)/shard_map/pallas_call | solution.py:169
  170.3 0.0 copy-done.5
  170.3 0.7 pad_add_fusion.1
  171.1 0.1 reshape.39
  171.2 0.0 copy-start.1
  171.2 0.0 all-to-all-done.5
  171.2 0.0 collective-permute-done.1
  171.2 19.2 %all-gather.2 = f32[16,34,256]{2,1,0:T(8,128)S(1)} all-gather(f32[1,34,256]{2,1,0:T(8,128)S(1)} %maximum_bitcast_fusion), channel_id=2, replica_groups=mesh['z'=8,'x'=4,'y'=8,'core'=2] {'y','core'}, dimensions={0}, use_global_device_ids=true | all-gather | bytes 591872 | tf_op jit(solution)/shard_map/all_gather | solution.py:245
  190.5 0.7 slice.53
  191.3 0.0 copy-done.1
  191.3 0.3 fusion.12
  191.6 0.6 copy-done.3
  192.2 0.4 fusion.13
  192.6 0.0 copy-start.2
  192.6 0.4 convolution_subtract_fusion.1
  193.0 0.4 fusion.14
  193.4 0.1 copy-done.2
  193.5 1.8 convolution_subtract_fusion
  (12 shorter events, 0.3 us)
Async XLA Ops:
  0.0 22.4 %copy-start = (f32[288,576]{1,0:T(8,128)S(1)}, f32[288,576]{1,0:T(8,128)}, u32[]{:S(2)}) copy-start(f32[288,576]{1,0:T(8,128)} %param.3) | copy-start | bytes 1990660
  51.7 28.1 %copy-start.7 = (f32[18,256]{1,0:T(8,128)S(1)}, f32[18,256]{1,0:T(8,128)}, u32[]{:S(2)}) copy-start(f32[18,256]{1,0:T(8,128)} %param.2) | copy-start | bytes 55300
  75.9 16.4 %all-to-all-start.2 = ((f32[32,16,256]{2,1,0:T(8,128)}), f32[32,16,256]{2,1,0:T(8,128)S(1)}, u32[]{:S(2)}, u32[]{:S(2)}) async-start(f32[32,16,256]{2,1,0:T(8,128)} %broadcast_in_dim.21), calls=%async_computation.2 | async-start | bytes 1048576 | tf_op jit(solution)/shard_map/all_to_all | solution.py:203
  79.8 24.9 %collective-permute-start = (f32[18,256]{1,0:T(8,128)S(1)}, f32[18,256]{1,0:T(8,128)S(1)}, u32[]{:S(2)}, u32[]{:S(2)}) collective-permute-start(f32[18,256]{1,0:T(8,128)S(1)} %copy-done.7), channel_id=1, source_target_pairs={{0,0},{1,64},{2,128},{3,192},{4,256},{5,320},{6,384},{7,448},{8,16... | collective-permute-start | bytes 55304 | tf_op jit(solution)/shard_map/ppermute | solution.py:215
  120.4 16.1 %copy-start.4 = (f32[256,256]{1,0:T(8,128)S(1)}, f32[256,256]{1,0:T(8,128)}, u32[]{:S(2)}) copy-start(f32[256,256]{1,0:T(8,128)} %get-tuple-element.7.upper_ref) | copy-start | bytes 786436
  121.5 15.8 %all-to-all-start.4 = ((f32[4,8,36,256]{3,1,2,0:T(8,128)}), f32[4,8,36,256]{3,1,2,0:T(8,128)S(1)}, u32[]{:S(2)}, u32[]{:S(2)}) async-start(f32[4,8,36,256]{3,1,2,0:T(8,128)} %broadcast_in_dim.23), calls=%async_computation.4 | async-start | bytes 2359296 | tf_op jit(solution)/shard_map/all_to_all | solution.py:207
  125.0 46.2 %collective-permute-start.1 = (f32[18,256]{1,0:T(8,128)S(1)}, f32[18,256]{1,0:T(8,128)S(1)}, u32[]{:S(2)}, u32[]{:S(2)}) collective-permute-start(f32[18,256]{1,0:T(8,128)S(1)} %convolution_add_fusion), channel_id=1, source_target_pairs={{0,0},{64,1},{128,2},{192,3},{256,4},{320,5},{384,6},{448,7},{16,8... | collective-permute-start | bytes 55304 | tf_op jit(solution)/shard_map/ppermute | solution.py:238
  138.4 0.9 copy-start.6
  144.2 27.0 %all-to-all-start.5 = ((f32[16,16,256]{2,1,0:T(8,128)}), f32[16,16,256]{2,1,0:T(8,128)S(1)}, u32[]{:S(2)}, u32[]{:S(2)}) async-start(f32[16,16,256]{2,1,0:T(8,128)} %fusion.11), calls=%async_computation.5 | async-start | bytes 524288 | tf_op jit(solution)/shard_map/all_to_all | solution.py:244
  156.8 13.5 %copy-start.5 = (f32[256,256]{1,0:T(8,128)S(1)}, f32[256,256]{1,0:T(8,128)}, u32[]{:S(2)}) copy-start(f32[256,256]{1,0:T(8,128)} %get-tuple-element.13) | copy-start | bytes 786436
  171.2 20.1 %copy-start.1 = (f32[256,256]{1,0:T(8,128)S(1)}, f32[256,256]{1,0:T(8,128)}, u32[]{:S(2)}) copy-start(f32[256,256]{1,0:T(8,128)} %shard_map.29) | copy-start | bytes 786436
  191.2 0.9 copy-start.3
  192.6 1.0 copy-start.2

commit v3 on v2

--- a/solution.py
+++ b/solution.py
@@ -30,12 +30,11 @@
     return jnp.dot(a, b, precision=precision, preferred_element_type=jnp.float32)
 
 
-def load_tiles(refs, at, block):
-    out = []
-    for ref in refs:
-        for lane in range(0, ref.shape[1], LANE):
-            out.append([ref[at + t : at + t + SUB, lane : lane + LANE] for t in range(0, block, SUB)])
-    return out
+def load_tiles(ref, at, block, lanes):
+    return [
+        [ref[at + t : at + t + SUB, lane : lane + LANE] for t in range(0, block, SUB)]
+        for lane in lanes
+    ]
 
 
 def spread_lane(tile, lane):
@@ -47,7 +46,7 @@
 
 
 def chol_group(parts, group, at, sub_ids):
-    part, lane = divmod(at + group * SUB, LANE)
+    part, lane = 0, (at + group * SUB) % LANE
     count = len(parts[0])
     cols = [spread_lane(parts[part][group], lane + k) for k in range(SUB)]
     entry = [[spread_row(cols[k], i) if i >= k else None for k in range(SUB)] for i in range(SUB)]
@@ -79,7 +78,7 @@
 
 
 def inv_group(parts, group, at, sub_ids):
-    part, lane = divmod(at + group * SUB, LANE)
+    part, lane = 0, (at + group * SUB) % LANE
     count = len(parts[0])
     cols = [spread_lane(parts[part][group], lane + k) for k in range(SUB)]
     entry = [[spread_row(cols[k], i) for k in range(SUB)] for i in range(SUB)]
@@ -112,69 +111,88 @@
     return jnp.concatenate([jnp.concatenate(p, 0) for p in parts], 1)
 
 
-def chol_body(block, gram_ref, upper_ref, linv_ref, schur):
-    n = gram_ref.shape[0]
-    half = n // LANE
-    schur[...] = gram_ref[...]
-    row_ids = lax.broadcasted_iota(jnp.int32, (n, n), 0)
-    col_ids = lax.broadcasted_iota(jnp.int32, (n, n), 1)
-    linv_ref[...] = jnp.where(row_ids == col_ids, 1.0, 0.0).astype(jnp.float32)
-    sub_ids = lax.broadcasted_iota(jnp.int32, (SUB, LANE), 0)
-    brow = lax.broadcasted_iota(jnp.int32, (block, n), 0)
-    bcol = lax.broadcasted_iota(jnp.int32, (block, n), 1)
-    for at in range(0, n, block):
-        here = pl.ds(at, block)
-        parts = load_tiles((schur, linv_ref), at, block)
-        for group in range(block // SUB):
-            chol_group(parts, group, at, sub_ids)
-        upper = jnp.where(bcol >= brow + at, join(parts[:half]), 0.0)
-        lower = join(parts[half:])
-        upper_ref[here, :] = upper
-        linv_ref[here, :] = lower
-        if at + block < n:
-            rest = pl.ds(at + block, n - at - block)
-            right = upper[:, at + block :]
-            schur[rest, :] = schur[rest, :] - tdot(right, upper)
-            linv_ref[rest, :] = linv_ref[rest, :] - tdot(right, lower)
-
-
-def inv_body(block, upper_ref, linv_ref, top_ref, kmat_ref, left):
-    n = top_ref.shape[0]
-    half = n // LANE
-    left[...] = top_ref[...] + upper_ref[...]
-    kmat_ref[...] = linv_ref[...]
+def chol_body(block, shared_ref, ap_ref, ae_ref, p_ref, upper_ref, copies_ref, schur):
+    n = upper_ref.shape[0]
+    piece = ap_ref.shape[0]
+    schur[...] = shared_ref[:, : n // shared_ref.shape[0], :].reshape(n, n)
+    upper_ref[...] = jnp.zeros((n, n), jnp.float32)
     sub_ids = lax.broadcasted_iota(jnp.int32, (SUB, LANE), 0)
     for at in range(0, n, block):
         here = pl.ds(at, block)
-        parts = load_tiles((left, kmat_ref), at, block)
+        base = at // LANE * LANE
+        parts = load_tiles(schur, at, block, range(base, n, LANE))
+        for group in range(block // SUB):
+            chol_group(parts, group, at, sub_ids)
+        rows = lax.broadcasted_iota(jnp.int32, (block, n - base), 0) + at
+        cols = lax.broadcasted_iota(jnp.int32, (block, n - base), 1) + base
+        upper = jnp.where(cols >= rows, join(parts), 0.0)
+        upper_ref[here, base:] = upper
+        after = at + block
+        if after < n:
+            rest = pl.ds(after, n - after)
+            keep = after // LANE * LANE
+            update = tdot(upper[:, after - base :], upper[:, keep - base :])
+            schur[rest, keep:] = schur[rest, keep:] - update
+    y_far = ap_ref[...] + dot(ae_ref[...], upper_ref[...])
+    for peer in range(copies_ref.shape[0]):
+        copies_ref[peer, :piece, :] = y_far
+        copies_ref[peer, piece:, :] = p_ref[...]
+
+
+def inv_body(block, shared_ref, upper_ref, kmat_ref, left):
+    n = upper_ref.shape[0]
+    g_rows = n // shared_ref.shape[0]
+    gram = shared_ref[:, :g_rows, :].reshape(n, n)
+    top = shared_ref[:, g_rows:, :].reshape(n, n)
+    left[...] = gram + tdot(upper_ref[...], top)
+    row_ids = lax.broadcasted_iota(jnp.int32, (n, n), 0)
+    col_ids = lax.broadcasted_iota(jnp.int32, (n, n), 1)
+    kmat_ref[...] = jnp.where(row_ids == col_ids, 1.0, 0.0).astype(jnp.float32)
+    sub_ids = lax.broadcasted_iota(jnp.int32, (SUB, LANE), 0)
+    for at in range(0, n, block):
+        here = pl.ds(at, block)
+        base = at // LANE * LANE
+        done = base + LANE
+        parts = load_tiles(left, at, block, range(base, n, LANE))
+        split = len(parts)
+        parts += load_tiles(kmat_ref, at, block, range(0, done, LANE))
         for group in range(block // SUB):
             inv_group(parts, group, at, sub_ids)
-        keep = join(parts[:half])
-        out = join(parts[half:])
-        left[here, :] = keep
-        kmat_ref[here, :] = out
+        keep = join(parts[:split])
+        out = join(parts[split:])
+        left[here, base:] = keep
+        kmat_ref[here, :done] = out
         for lo, hi in ((at + block, n), (0, at)):
             if hi > lo:
                 other = pl.ds(lo, hi - lo)
                 column = left[other, at : at + block]
                 if at + block < n:
-                    left[other, :] = left[other, :] - dot(column, keep)
-                kmat_ref[other, :] = kmat_ref[other, :] - dot(column, out)
-
-
-def local_call(body, outs, scratch, block, *args):
-    n = args[0].shape[0]
-    shape = jax.ShapeDtypeStruct((n, n), jnp.float32)
+                    left[other, base:] = left[other, base:] - dot(column, keep)
+                kmat_ref[other, :done] = kmat_ref[other, :done] - dot(column, out)
+
+
+def pair_body(both_ref, first_ref, v_ref, y_ref, c_ref):
+    count, twice, _ = both_ref.shape
+    piece = twice // 2
+    for k in range(count):
+        y_ref[k * piece : (k + 1) * piece, :] = both_ref[k, :piece, :]
+        v_ref[k * piece : (k + 1) * piece, :] = both_ref[k, piece:, :]
+    n = first_ref.shape[0]
+    v_ref[:n, :] = v_ref[:n, :] + first_ref[...]
+    c_ref[...] = tdot(v_ref[...], y_ref[...])
+
+
+def local_call(body, outs, scratch, flops, *args):
     vmem = pl.BlockSpec(memory_space=pltpu.VMEM)
+    shapes = tuple(jax.ShapeDtypeStruct(out, jnp.float32) for out in outs)
+    moved = sum(4 * int(np.prod(shape)) for shape in outs + [arg.shape for arg in args])
     return pl.pallas_call(
-        functools.partial(body, block),
-        out_shape=(shape,) * outs,
+        body,
+        out_shape=shapes,
         in_specs=[vmem] * len(args),
-        out_specs=(vmem,) * outs,
-        scratch_shapes=[pltpu.VMEM((n, n), jnp.float32)] * scratch,
-        cost_estimate=pl.CostEstimate(
-            flops=16_000_000_000, bytes_accessed=4 * n * n * (outs + len(args)), transcendentals=n
-        ),
+        out_specs=(vmem,) * len(outs),
+        scratch_shapes=[pltpu.VMEM(shape, jnp.float32) for shape in scratch],
+        cost_estimate=pl.CostEstimate(flops=flops, bytes_accessed=moved, transcendentals=256),
     )(*args)
 
 
@@ -201,11 +219,6 @@
     def share_row(part):
         copies = jnp.broadcast_to(part, (n_row, *part.shape))
         return lax.all_to_all(copies, ROW, 0, 0)
-
-    def share_twice(part):
-        ring = lax.all_to_all(jnp.broadcast_to(part, (DEPTH, *part.shape)), "z", 0, 0)
-        full = lax.all_to_all(jnp.broadcast_to(ring, (WIDTH, *ring.shape)), "x", 0, 0)
-        return full.reshape(n_row, *part.shape)
 
     def sum_twice(stack):
         stack = stack.reshape(WIDTH, DEPTH, *stack.shape[1:])
@@ -224,24 +237,30 @@
     moved = sum_twice(jnp.concatenate(stacked, 1))
     at = 2 * piece
     ap_far, ae_far = moved[:piece], moved[piece:at]
-    both = share_row(moved[at:])
-    gram = both[:, :g_rows].reshape(width, width)
-    top = both[:, g_rows:].reshape(width, width)
-
-    upper, linv = local_call(chol_body, 2, 1, 64, gram)
-    (kmat,) = local_call(inv_body, 1, 1, 64, upper, linv, top)
-
-    y_far = ap_far + dot(ae_far, upper, HIGH)
-    both = share_twice(jnp.concatenate([y_far, p_far], 0))
-    y_col = both[:, :piece].reshape(col_rows, width)
-    p_col = both[:, piece:].reshape(col_rows, width)
-    y_own = lax.ppermute(y_far, EVERY, back)
+    shared = share_row(moved[at:])
+    square = (width, width)
+    upper, copies = local_call(
+        functools.partial(chol_body, 64),
+        [square, (DEPTH, at, width)],
+        [square],
+        10_000_000_000,
+        *(shared, ap_far, ae_far, p_far),
+    )
+    (kmat,) = local_call(
+        functools.partial(inv_body, 64), [square], [square], 14_000_000_000, shared, upper
+    )
+
+    ring = lax.all_to_all(copies, "z", 0, 0)
+    both = lax.all_to_all(jnp.broadcast_to(ring, (WIDTH, *ring.shape)), "x", 0, 0)
+    both = both.reshape(n_row, at, width)
+    y_own = lax.ppermute(copies[0, :piece], EVERY, back)
     first_row = jnp.where(first, upper, 0.0)
     first_col = jnp.where(col_at == 0, upper, 0.0)
     v_row = p_row + jnp.pad(first_row, ((0, row_rows - width), (0, 0)))
-    v_col = p_col + jnp.pad(first_col, ((0, col_rows - width), (0, 0)))
-    c_part = tdot(v_col, y_col, HIGH).reshape(n_col, c_rows, width)
-    c_part = lax.all_to_all(c_part, COL, 0, 0)
+    v_col, y_col, c_part = local_call(
+        pair_body, [(col_rows, width)] * 2 + [square], [], 2_000_000_000, both, first_col
+    )
+    c_part = lax.all_to_all(c_part.reshape(n_col, c_rows, width), COL, 0, 0)
     last = lax.all_gather(jnp.concatenate([jnp.sum(c_part, 0), y_own], 0), COL, axis=0)
     core = last[:, :c_rows].reshape(width, width)
     y_row = last[:, c_rows:].reshape(row_rows, width)

time: 196 us -> 196 us (level)
  matrix products: 9.09 us -> 5.74 us
  Pallas kernels: 24 us -> 27.2 us
  local copies, waits for them, and re-layouts: 10.2 us -> 7.11 us
  starting transfers between devices: 37.5 us -> 40.5 us
    all_to_all x1, waiting for transfers between devices: 6.44 us -> 2.92 us  [share_row(): return lax.all_to_all(copies, ROW, 0, 0)]
    pallas_call x2 -> x3, Pallas kernels: 24 us -> 27.2 us  [local_call(): pl.pallas_call(body, out_shape=shapes, in_specs=[vmem] * len(args), out_s...]
    ppermute x1, waiting for transfers between devices: 0.01 us -> 2.88 us  [on_device(): p_far = lax.ppermute(panel, EVERY, moves)]
    all_to_all x2, starting transfers between devices: 16.1 us -> 18.5 us  [the longest x1 15 us: on_device(): c_part = lax.all_to_all(c_part.reshape(n_col, c_rows, width), COL, 0, 0)]
    dot_general x4 -> x3, matrix products: 5.12 us -> 2.87 us  [tdot(): lax.dot_general(a, b, (((0,), (0,)), ((), ())), precision=precision, pref...]
    slice x4 -> x2, local copies, waits for them, and re-layouts: 2.73 us -> 0.63 us  [the longest x1 0.62 us: on_device(): ap_far, ae_far = (moved[:piece], moved[piece:at])]
  transfers between devices with their start and end apart: 5 -> 5, of which waited for: 1 -> 2; matrix products, arithmetic and copies ran while one was open for 5% -> 2% of each run, Pallas kernels for 12% -> 9%
where the time goes in v3:
time: 196 us; the launch traced here: 195 us
  blocking collectives  106 us (54%)
  starting transfers between devices  40.5 us (21%)
  Pallas kernels  27.2 us (14%)
  local copies, waits for them, and re-layouts  7.11 us (4%)
  waiting for transfers between devices  5.81 us (3%)
  matrix products  5.74 us (3%)
  other arithmetic  2.22 us (1%)
    pallas_call x3, Pallas kernels, local_call(): pl.pallas_call(body, out_shape=shapes, in_specs=[vmem] * len(args), out_s...  27.2 us
    all_to_all x1, blocking collectives, sum_twice(): stack = jnp.sum(lax.all_to_all(stack, 'x', 0, 0), 0)  24.3 us
    all_to_all x1, blocking collectives, sum_twice(): return jnp.sum(lax.all_to_all(stack, 'z', 0, 0), 0)  23.3 us
    all_gather x1, blocking collectives, on_device(): p_row = lax.all_gather(panel, COL, axis=0, tiled=True)  22.3 us
    all_gather x1, blocking collectives, on_device(): lax.all_gather(jnp.concatenate([jnp.sum(c_part, 0), y_own], 0), COL, axis=0)  19.2 us
    all_to_all x1, blocking collectives, on_device(): ring = lax.all_to_all(copies, 'z', 0, 0)  17.3 us
    all_to_all x1, starting transfers between devices, on_device(): c_part = lax.all_to_all(c_part.reshape(n_col, c_rows, width), COL, 0, 0)  15 us
    ppermute x1, starting transfers between devices, on_device(): y_own = lax.ppermute(copies[0, :piece], EVERY, back)  12 us
  transfers between devices with their start and end apart: 5, of which 2 were waited for; matrix products, arithmetic and copies ran while one was open for 2% of the time, Pallas kernels for 9%

profile of v3, /device:TPU:1, one launch (start us, length us, event | category | flops | bytes accessed | tf_op | source)
XLA Modules:
  0.0 195.3 jit_solution(7627569321503104796)
XLA Ops:
  0.0 0.0 copy-start
  0.0 22.3 %all-gather.1 = f32[16,18,256]{2,1,0:T(8,128)S(1)} all-gather(f32[1,18,256]{2,1,0:T(8,128)} %bitcast.28), channel_id=1, replica_groups=mesh['z'=8,'x'=4,'y'=8,'core'=2] {'y','core'}, dimensions={0}, use_global_device_ids=true | all-gather | bytes 313344 | tf_op jit(solution)/shard_map/all_gather | solution.py:229
  22.4 1.5 fusion.11
  23.9 0.0 copy-done
  24.0 1.0 fusion.10
  25.0 0.2 copy.13
  25.2 0.1 concatenate.22
  25.3 0.1 concatenate.21
  25.3 1.2 pad_maximum_fusion
  26.5 0.5 copy.14
  27.1 24.3 %all_to_all.30 = f32[4,8,52,256]{3,1,2,0:T(8,128)S(1)} all-to-all(f32[4,8,52,256]{3,1,2,0:T(8,128)S(1)} %copy.14), channel_id=1, replica_groups=mesh['z'=8,'x'=4,'y'=8,'core'=2] {'x'}, dimensions={0} | all-to-all | bytes 3407872 | tf_op jit(solution)/shard_map/all_to_all | solution.py:225
  51.4 0.1 reduce_sum.27
  51.5 0.1 copy.15
  51.7 0.0 copy-start.6
  51.7 23.3 %all_to_all.31 = f32[8,52,256]{2,1,0:T(8,128)S(1)} all-to-all(f32[8,52,256]{2,1,0:T(8,128)S(1)} %copy.15), channel_id=1, replica_groups=mesh['z'=8,'x'=4,'y'=8,'core'=2] {'z'}, dimensions={0} | all-to-all | bytes 851968 | tf_op jit(solution)/shard_map/all_to_all | solution.py:226
  75.0 0.9 broadcast_in_dim.18
  75.9 3.9 %all-to-all-start.2 = ((f32[32,16,256]{2,1,0:T(8,128)}), f32[32,16,256]{2,1,0:T(8,128)S(1)}, u32[]{:S(2)}, u32[]{:S(2)}) async-start(f32[32,16,256]{2,1,0:T(8,128)} %broadcast_in_dim.18), calls=%async_computation.2 | async-start | bytes 1048576 | tf_op jit(solution)/shard_map/all_to_all | solution.py:221
  79.8 0.0 copy-done.6
  79.8 6.1 %collective-permute-start = (f32[18,256]{1,0:T(8,128)S(1)}, f32[18,256]{1,0:T(8,128)S(1)}, u32[]{:S(2)}, u32[]{:S(2)}) collective-permute-start(f32[18,256]{1,0:T(8,128)S(1)} %copy-done.6), channel_id=1, source_target_pairs={{0,0},{1,64},{2,128},{3,192},{4,256},{5,320},{6,384},{7,448},{8,16... | collective-permute-start | bytes 55304 | tf_op jit(solution)/shard_map/ppermute | solution.py:228
  85.9 0.6 fusion.9
  86.5 2.9 %collective-permute-done.p_ref = f32[18,256]{1,0:T(8,128)S(1)} collective-permute-done((f32[18,256]{1,0:T(8,128)S(1)}, f32[18,256]{1,0:T(8,128)S(1)}, u32[]{:S(2)}, u32[]{:S(2)}) %collective-permute-start) | collective-permute-done | bytes 18464 | tf_op jit(solution)/shard_map/ppermute | solution.py:228
  89.4 0.0 copy-start.7
  89.4 2.9 %all-to-all-done.2.shared_ref = f32[32,16,256]{2,1,0:T(8,128)S(1)} async-done(((f32[32,16,256]{2,1,0:T(8,128)}), f32[32,16,256]{2,1,0:T(8,128)S(1)}, u32[]{:S(2)}, u32[]{:S(2)}) %all-to-all-start.2) | async-done | bytes 524320 | tf_op jit(solution)/shard_map/all_to_all | solution.py:221
  92.3 0.0 copy-start.4
  92.3 0.0 copy-done.7
  92.3 0.8 copy-done.4
  93.1 10.4 %shard_map.28 = (f32[256,256]{1,0:T(8,128)}, f32[8,36,256]{2,1,0:T(8,128)}) custom-call(f32[32,16,256]{2,1,0:T(8,128)} %copy-done.4, f32[18,256]{1,0:T(8,128)} %get-tuple-element.18.ap_ref, f32[18,256]{1,0:T(8,128)} %get-tuple-element.17.ae_ref, f32[18,256]{1,0:T(8,128)} %copy-done.7), custom_call_target="tpu_custom_call" | custom-call | flops 10000000000 | bytes 1136640 | tf_op jit(solution)/shard_map/pallas_call | solution.py:189
  103.5 17.3 %all_to_all.32 = f32[8,36,256]{2,1,0:T(8,128)S(1)} all-to-all(f32[8,36,256]{2,1,0:T(8,128)} %get-tuple-element.10), channel_id=1, replica_groups=mesh['z'=8,'x'=4,'y'=8,'core'=2] {'z'}, dimensions={0} | all-to-all | bytes 589824 | tf_op jit(solution)/shard_map/all_to_all | solution.py:253
  120.8 0.1 copy.16
  120.9 0.0 copy-start.5
  120.9 1.1 broadcast_in_dim.19
  122.0 3.5 %all-to-all-start.4 = ((f32[4,8,36,256]{3,1,2,0:T(8,128)}), f32[4,8,36,256]{3,1,2,0:T(8,128)S(1)}, u32[]{:S(2)}, u32[]{:S(2)}) async-start(f32[4,8,36,256]{3,1,2,0:T(8,128)} %broadcast_in_dim.19), calls=%async_computation.4 | async-start | bytes 2359296 | tf_op jit(solution)/shard_map/all_to_all | solution.py:254
  125.6 0.7 slice_bitcast_fusion
  126.3 12.0 %collective-permute-start.1 = (f32[18,256]{1,0:T(8,128)S(1)}, f32[18,256]{1,0:T(8,128)S(1)}, u32[]{:S(2)}, u32[]{:S(2)}) collective-permute-start(f32[18,256]{1,0:T(8,128)S(1)} %slice_bitcast_fusion), channel_id=1, source_target_pairs={{0,0},{64,1},{128,2},{192,3},{256,4},{320,5},{384,6},{448,7},{16,8... | collective-permute-start | bytes 55304 | tf_op jit(solution)/shard_map/ppermute | solution.py:256
  138.3 0.0 copy-done.5
  138.3 0.8 broadcast_select_fusion
  139.0 0.0 all-to-all-done.4
  139.0 1.5 copy.17
  140.5 3.1 %shard_map.29 = (f32[576,256]{1,0:T(8,128)}, f32[576,256]{1,0:T(8,128)}, f32[256,256]{1,0:T(8,128)}) custom-call(f32[32,36,256]{2,1,0:T(8,128)} %bitcast.23, f32[256,256]{1,0:T(8,128)} %get-tuple-element.16.first_ref), custom_call_target="tpu_custom_call" | custom-call | flops 2000000000 | bytes 2883584 | tf_op jit(solution)/shard_map/pallas_call | solution.py:189
  143.6 15.0 %all-to-all-start.5 = ((f32[16,16,256]{2,1,0:T(8,128)}), f32[16,16,256]{2,1,0:T(8,128)S(1)}, u32[]{:S(2)}, u32[]{:S(2)}) async-start(f32[16,16,256]{2,1,0:T(8,128)} %bitcast.27), calls=%async_computation.5 | async-start | bytes 524288 | tf_op jit(solution)/shard_map/all_to_all | solution.py:263
  158.6 13.7 %shard_map.30 = f32[256,256]{1,0:T(8,128)} custom-call(f32[32,16,256]{2,1,0:T(8,128)} %copy-done.4, f32[256,256]{1,0:T(8,128)} %get-tuple-element.11.upper_ref), custom_call_target="tpu_custom_call" | custom-call | flops 14000000000 | bytes 1048576 | tf_op jit(solution)/shard_map/pallas_call | solution.py:189
  172.4 0.0 copy-start.2
  172.4 0.0 all-to-all-done.5
  172.4 0.0 collective-permute-done.1
  172.4 19.2 %all-gather.2 = f32[16,34,256]{2,1,0:T(8,128)S(1)} all-gather(f32[1,34,256]{2,1,0:T(8,128)S(1)} %maximum_bitcast_fusion), channel_id=2, replica_groups=mesh['z'=8,'x'=4,'y'=8,'core'=2] {'y','core'}, dimensions={0}, use_global_device_ids=true | all-gather | bytes 591872 | tf_op jit(solution)/shard_map/all_gather | solution.py:264
  191.6 0.0 copy-start.1
  191.8 0.0 copy-start.3
  191.8 0.0 copy-done.2
  191.8 0.4 fusion.13
  192.2 0.3 fusion.12
  192.5 0.2 copy-done.1
  192.7 0.4 fusion.14
  193.1 0.0 copy-done.3
  193.1 0.4 fusion.6
  193.6 1.8 convolution_subtract_fusion
  (11 shorter events, 0.3 us)
Async XLA Ops:
  0.0 23.9 %copy-start = (f32[288,576]{1,0:T(8,128)S(1)}, f32[288,576]{1,0:T(8,128)}, u32[]{:S(2)}) copy-start(f32[288,576]{1,0:T(8,128)} %param.3) | copy-start | bytes 1990660
  51.7 28.1 %copy-start.6 = (f32[18,256]{1,0:T(8,128)S(1)}, f32[18,256]{1,0:T(8,128)}, u32[]{:S(2)}) copy-start(f32[18,256]{1,0:T(8,128)} %param.2) | copy-start | bytes 55300
  75.9 16.4 %all-to-all-start.2 = ((f32[32,16,256]{2,1,0:T(8,128)}), f32[32,16,256]{2,1,0:T(8,128)S(1)}, u32[]{:S(2)}, u32[]{:S(2)}) async-start(f32[32,16,256]{2,1,0:T(8,128)} %broadcast_in_dim.18), calls=%async_computation.2 | async-start | bytes 1048576 | tf_op jit(solution)/shard_map/all_to_all | solution.py:221
  79.8 9.6 %collective-permute-start = (f32[18,256]{1,0:T(8,128)S(1)}, f32[18,256]{1,0:T(8,128)S(1)}, u32[]{:S(2)}, u32[]{:S(2)}) collective-permute-start(f32[18,256]{1,0:T(8,128)S(1)} %copy-done.6), channel_id=1, source_target_pairs={{0,0},{1,64},{2,128},{3,192},{4,256},{5,320},{6,384},{7,448},{8,16... | collective-permute-start | bytes 55304 | tf_op jit(solution)/shard_map/ppermute | solution.py:228
  89.4 2.9 %copy-start.7 = (f32[18,256]{1,0:T(8,128)}, f32[18,256]{1,0:T(8,128)S(1)}, u32[]{:S(2)}) copy-start(f32[18,256]{1,0:T(8,128)S(1)} %collective-permute-done.p_ref) | copy-start | bytes 55300
  92.3 0.8 copy-start.4
  120.9 17.4 %copy-start.5 = (f32[256,256]{1,0:T(8,128)S(1)}, f32[256,256]{1,0:T(8,128)}, u32[]{:S(2)}) copy-start(f32[256,256]{1,0:T(8,128)} %get-tuple-element.11.upper_ref) | copy-start | bytes 786436
  122.0 17.0 %all-to-all-start.4 = ((f32[4,8,36,256]{3,1,2,0:T(8,128)}), f32[4,8,36,256]{3,1,2,0:T(8,128)S(1)}, u32[]{:S(2)}, u32[]{:S(2)}) async-start(f32[4,8,36,256]{3,1,2,0:T(8,128)} %broadcast_in_dim.19), calls=%async_computation.4 | async-start | bytes 2359296 | tf_op jit(solution)/shard_map/all_to_all | solution.py:254
  126.3 46.1 %collective-permute-start.1 = (f32[18,256]{1,0:T(8,128)S(1)}, f32[18,256]{1,0:T(8,128)S(1)}, u32[]{:S(2)}, u32[]{:S(2)}) collective-permute-start(f32[18,256]{1,0:T(8,128)S(1)} %slice_bitcast_fusion), channel_id=1, source_target_pairs={{0,0},{64,1},{128,2},{192,3},{256,4},{320,5},{384,6},{448,7},{16,8... | collective-permute-start | bytes 55304 | tf_op jit(solution)/shard_map/ppermute | solution.py:256
  143.6 28.8 %all-to-all-start.5 = ((f32[16,16,256]{2,1,0:T(8,128)}), f32[16,16,256]{2,1,0:T(8,128)S(1)}, u32[]{:S(2)}, u32[]{:S(2)}) async-start(f32[16,16,256]{2,1,0:T(8,128)} %bitcast.27), calls=%async_computation.5 | async-start | bytes 524288 | tf_op jit(solution)/shard_map/all_to_all | solution.py:263
  172.4 19.4 %copy-start.2 = (f32[256,256]{1,0:T(8,128)S(1)}, f32[256,256]{1,0:T(8,128)}, u32[]{:S(2)}) copy-start(f32[256,256]{1,0:T(8,128)} %shard_map.30) | copy-start | bytes 786436
  191.6 1.1 copy-start.1
  191.8 1.4 copy-start.3

commit v4 on v3

--- a/solution.py
+++ b/solution.py
@@ -172,11 +172,13 @@
 
 
 def pair_body(both_ref, first_ref, v_ref, y_ref, c_ref):
-    count, twice, _ = both_ref.shape
-    piece = twice // 2
-    for k in range(count):
-        y_ref[k * piece : (k + 1) * piece, :] = both_ref[k, :piece, :]
-        v_ref[k * piece : (k + 1) * piece, :] = both_ref[k, piece:, :]
+    groups, _, _ = both_ref.shape
+    piece = y_ref.shape[0] // (groups * DEPTH)
+    for k in range(groups * DEPTH):
+        start = k % DEPTH * 2 * piece
+        here = pl.ds(k * piece, piece)
+        y_ref[here, :] = both_ref[k // DEPTH, start : start + piece, :]
+        v_ref[here, :] = both_ref[k // DEPTH, start + piece : start + 2 * piece, :]
     n = first_ref.shape[0]
     v_ref[:n, :] = v_ref[:n, :] + first_ref[...]
     c_ref[...] = tdot(v_ref[...], y_ref[...])
@@ -250,9 +252,8 @@
         functools.partial(inv_body, 64), [square], [square], 14_000_000_000, shared, upper
     )
 
-    ring = lax.all_to_all(copies, "z", 0, 0)
+    ring = lax.all_to_all(copies, "z", 0, 0).reshape(DEPTH * at, width)
     both = lax.all_to_all(jnp.broadcast_to(ring, (WIDTH, *ring.shape)), "x", 0, 0)
-    both = both.reshape(n_row, at, width)
     y_own = lax.ppermute(copies[0, :piece], EVERY, back)
     first_row = jnp.where(first, upper, 0.0)
     first_col = jnp.where(col_at == 0, upper, 0.0)

time: 196 us -> 196 us (level)
  transfers between devices with their start and end apart: 5 -> 5, of which waited for: 2 -> 2; matrix products, arithmetic and copies ran while one was open for 2% -> 1% of each run, Pallas kernels for 9% -> 9%
where the time goes in v4:
time: 196 us; the launch traced here: 195 us
  blocking collectives  106 us (54%)
  starting transfers between devices  40.5 us (21%)
  Pallas kernels  27.2 us (14%)
  local copies, waits for them, and re-layouts  6.64 us (3%)
  waiting for transfers between devices  5.81 us (3%)
  matrix products  5.74 us (3%)
  other arithmetic  2.22 us (1%)
    pallas_call x3, Pallas kernels, local_call(): pl.pallas_call(body, out_shape=shapes, in_specs=[vmem] * len(args), out_s...  27.2 us
    all_to_all x1, blocking collectives, sum_twice(): stack = jnp.sum(lax.all_to_all(stack, 'x', 0, 0), 0)  24.3 us
    all_to_all x1, blocking collectives, sum_twice(): return jnp.sum(lax.all_to_all(stack, 'z', 0, 0), 0)  23.3 us
    all_gather x1, blocking collectives, on_device(): p_row = lax.all_gather(panel, COL, axis=0, tiled=True)  22.3 us
    all_gather x1, blocking collectives, on_device(): lax.all_gather(jnp.concatenate([jnp.sum(c_part, 0), y_own], 0), COL, axis=0)  19.2 us
    all_to_all x1, blocking collectives, on_device(): ring = lax.all_to_all(copies, 'z', 0, 0).reshape(DEPTH * at, width)  17.3 us
    all_to_all x1, starting transfers between devices, on_device(): c_part = lax.all_to_all(c_part.reshape(n_col, c_rows, width), COL, 0, 0)  15 us
    ppermute x1, starting transfers between devices, on_device(): y_own = lax.ppermute(copies[0, :piece], EVERY, back)  12 us
  transfers between devices with their start and end apart: 5, of which 2 were waited for; matrix products, arithmetic and copies ran while one was open for 1% of the time, Pallas kernels for 9%

profile of v4, /device:TPU:1, one launch (start us, length us, event | category | flops | bytes accessed | tf_op | source)
XLA Modules:
  0.0 194.8 jit_solution(12425049057293108234)
XLA Ops:
  0.0 0.0 copy-start
  0.0 22.3 %all-gather.1 = f32[16,18,256]{2,1,0:T(8,128)S(1)} all-gather(f32[1,18,256]{2,1,0:T(8,128)} %bitcast.26), channel_id=1, replica_groups=mesh['z'=8,'x'=4,'y'=8,'core'=2] {'y','core'}, dimensions={0}, use_global_device_ids=true | all-gather | bytes 313344 | tf_op jit(solution)/shard_map/all_gather | solution.py:231
  22.4 1.5 fusion.11
  23.9 0.0 copy-done
  24.0 1.0 fusion.10
  25.0 0.2 copy.9
  25.2 0.1 concatenate.22
  25.3 0.1 concatenate.21
  25.3 1.2 pad_maximum_fusion
  26.5 0.5 copy.10
  27.1 24.3 %all_to_all.30 = f32[4,8,52,256]{3,1,2,0:T(8,128)S(1)} all-to-all(f32[4,8,52,256]{3,1,2,0:T(8,128)S(1)} %copy.10), channel_id=1, replica_groups=mesh['z'=8,'x'=4,'y'=8,'core'=2] {'x'}, dimensions={0} | all-to-all | bytes 3407872 | tf_op jit(solution)/shard_map/all_to_all | solution.py:227
  51.4 0.1 reduce_sum.27
  51.5 0.0 copy-start.7
  51.5 0.1 copy.11
  51.7 23.3 %all_to_all.31 = f32[8,52,256]{2,1,0:T(8,128)S(1)} all-to-all(f32[8,52,256]{2,1,0:T(8,128)S(1)} %copy.11), channel_id=1, replica_groups=mesh['z'=8,'x'=4,'y'=8,'core'=2] {'z'}, dimensions={0} | all-to-all | bytes 851968 | tf_op jit(solution)/shard_map/all_to_all | solution.py:228
  75.0 0.9 broadcast_in_dim.18
  75.9 3.9 %all-to-all-start.2 = ((f32[32,16,256]{2,1,0:T(8,128)}), f32[32,16,256]{2,1,0:T(8,128)S(1)}, u32[]{:S(2)}, u32[]{:S(2)}) async-start(f32[32,16,256]{2,1,0:T(8,128)} %broadcast_in_dim.18), calls=%async_computation.2 | async-start | bytes 1048576 | tf_op jit(solution)/shard_map/all_to_all | solution.py:223
  79.8 0.0 copy-done.7
  79.8 6.1 %collective-permute-start = (f32[18,256]{1,0:T(8,128)S(1)}, f32[18,256]{1,0:T(8,128)S(1)}, u32[]{:S(2)}, u32[]{:S(2)}) collective-permute-start(f32[18,256]{1,0:T(8,128)S(1)} %copy-done.7), channel_id=1, source_target_pairs={{0,0},{1,64},{2,128},{3,192},{4,256},{5,320},{6,384},{7,448},{8,16... | collective-permute-start | bytes 55304 | tf_op jit(solution)/shard_map/ppermute | solution.py:230
  85.9 0.6 fusion.9
  86.5 2.9 %collective-permute-done.p_ref = f32[18,256]{1,0:T(8,128)S(1)} collective-permute-done((f32[18,256]{1,0:T(8,128)S(1)}, f32[18,256]{1,0:T(8,128)S(1)}, u32[]{:S(2)}, u32[]{:S(2)}) %collective-permute-start) | collective-permute-done | bytes 18464 | tf_op jit(solution)/shard_map/ppermute | solution.py:230
  89.4 0.0 copy-start.8
  89.4 2.9 %all-to-all-done.2.shared_ref = f32[32,16,256]{2,1,0:T(8,128)S(1)} async-done(((f32[32,16,256]{2,1,0:T(8,128)}), f32[32,16,256]{2,1,0:T(8,128)S(1)}, u32[]{:S(2)}, u32[]{:S(2)}) %all-to-all-start.2) | async-done | bytes 524320 | tf_op jit(solution)/shard_map/all_to_all | solution.py:223
  92.3 0.0 copy-start.5
  92.3 0.0 copy-done.8
  92.3 0.8 copy-done.5
  93.1 10.4 %shard_map.28 = (f32[256,256]{1,0:T(8,128)}, f32[8,36,256]{2,1,0:T(8,128)}) custom-call(f32[32,16,256]{2,1,0:T(8,128)} %copy-done.5, f32[18,256]{1,0:T(8,128)} %get-tuple-element.18.ap_ref, f32[18,256]{1,0:T(8,128)} %get-tuple-element.17.ae_ref, f32[18,256]{1,0:T(8,128)} %copy-done.8), custom_call_target="tpu_custom_call" | custom-call | flops 10000000000 | bytes 1136640 | tf_op jit(solution)/shard_map/pallas_call | solution.py:191
  103.5 17.3 %all_to_all.32 = f32[8,36,256]{2,1,0:T(8,128)S(1)} all-to-all(f32[8,36,256]{2,1,0:T(8,128)} %get-tuple-element.10), channel_id=1, replica_groups=mesh['z'=8,'x'=4,'y'=8,'core'=2] {'z'}, dimensions={0} | all-to-all | bytes 589824 | tf_op jit(solution)/shard_map/all_to_all | solution.py:255
  120.8 0.0 copy-start.6
  120.8 1.1 broadcast_in_dim.19
  122.0 3.5 %all-to-all-start.4 = ((f32[4,288,256]{2,1,0:T(8,128)}), f32[4,288,256]{2,1,0:T(8,128)S(1)}, u32[]{:S(2)}, u32[]{:S(2)}) async-start(f32[4,288,256]{2,1,0:T(8,128)} %broadcast_in_dim.19), calls=%async_computation.4 | async-start | bytes 2359296 | tf_op jit(solution)/shard_map/all_to_all | solution.py:256
  125.5 0.7 slice_bitcast_fusion
  126.3 12.0 %collective-permute-start.1 = (f32[18,256]{1,0:T(8,128)S(1)}, f32[18,256]{1,0:T(8,128)S(1)}, u32[]{:S(2)}, u32[]{:S(2)}) collective-permute-start(f32[18,256]{1,0:T(8,128)S(1)} %slice_bitcast_fusion), channel_id=1, source_target_pairs={{0,0},{64,1},{128,2},{192,3},{256,4},{320,5},{384,6},{448,7},{16,8... | collective-permute-start | bytes 55304 | tf_op jit(solution)/shard_map/ppermute | solution.py:257
  138.2 0.0 copy-done.6
  138.2 0.8 broadcast_select_fusion
  139.0 0.0 all-to-all-done.4.both_ref
  139.0 0.0 copy-start.3
  139.0 1.0 copy-done.3
  140.0 3.0 %shard_map.29 = (f32[576,256]{1,0:T(8,128)}, f32[576,256]{1,0:T(8,128)}, f32[256,256]{1,0:T(8,128)}) custom-call(f32[4,288,256]{2,1,0:T(8,128)} %copy-done.3, f32[256,256]{1,0:T(8,128)} %get-tuple-element.16.first_ref), custom_call_target="tpu_custom_call" | custom-call | flops 2000000000 | bytes 2883584 | tf_op jit(solution)/shard_map/pallas_call | solution.py:191
  143.0 15.0 %all-to-all-start.5 = ((f32[16,16,256]{2,1,0:T(8,128)}), f32[16,16,256]{2,1,0:T(8,128)S(1)}, u32[]{:S(2)}, u32[]{:S(2)}) async-start(f32[16,16,256]{2,1,0:T(8,128)} %bitcast.25), calls=%async_computation.5 | async-start | bytes 524288 | tf_op jit(solution)/shard_map/all_to_all | solution.py:264
  158.0 13.8 %shard_map.30 = f32[256,256]{1,0:T(8,128)} custom-call(f32[32,16,256]{2,1,0:T(8,128)} %copy-done.5, f32[256,256]{1,0:T(8,128)} %get-tuple-element.11.upper_ref), custom_call_target="tpu_custom_call" | custom-call | flops 14000000000 | bytes 1048576 | tf_op jit(solution)/shard_map/pallas_call | solution.py:191
  171.8 0.0 copy-start.2
  171.8 0.0 all-to-all-done.5
  171.9 0.0 collective-permute-done.1
  171.9 19.2 %all-gather.2 = f32[16,34,256]{2,1,0:T(8,128)S(1)} all-gather(f32[1,34,256]{2,1,0:T(8,128)S(1)} %maximum_bitcast_fusion), channel_id=2, replica_groups=mesh['z'=8,'x'=4,'y'=8,'core'=2] {'y','core'}, dimensions={0}, use_global_device_ids=true | all-gather | bytes 591872 | tf_op jit(solution)/shard_map/all_gather | solution.py:265
  191.1 0.0 copy-start.1
  191.2 0.0 copy-start.4
  191.2 0.0 copy-done.2
  191.2 0.4 fusion.13
  191.6 0.3 fusion.12
  191.9 0.3 copy-done.1
  192.2 0.4 fusion.14
  192.6 0.0 copy-done.4
  192.6 0.4 fusion.6
  193.0 1.8 convolution_subtract_fusion
  (12 shorter events, 0.3 us)
Async XLA Ops:
  0.0 23.9 %copy-start = (f32[288,576]{1,0:T(8,128)S(1)}, f32[288,576]{1,0:T(8,128)}, u32[]{:S(2)}) copy-start(f32[288,576]{1,0:T(8,128)} %param.3) | copy-start | bytes 1990660
  51.5 28.3 %copy-start.7 = (f32[18,256]{1,0:T(8,128)S(1)}, f32[18,256]{1,0:T(8,128)}, u32[]{:S(2)}) copy-start(f32[18,256]{1,0:T(8,128)} %param.2) | copy-start | bytes 55300
  75.9 16.4 %all-to-all-start.2 = ((f32[32,16,256]{2,1,0:T(8,128)}), f32[32,16,256]{2,1,0:T(8,128)S(1)}, u32[]{:S(2)}, u32[]{:S(2)}) async-start(f32[32,16,256]{2,1,0:T(8,128)} %broadcast_in_dim.18), calls=%async_computation.2 | async-start | bytes 1048576 | tf_op jit(solution)/shard_map/all_to_all | solution.py:223
  79.8 9.6 %collective-permute-start = (f32[18,256]{1,0:T(8,128)S(1)}, f32[18,256]{1,0:T(8,128)S(1)}, u32[]{:S(2)}, u32[]{:S(2)}) collective-permute-start(f32[18,256]{1,0:T(8,128)S(1)} %copy-done.7), channel_id=1, source_target_pairs={{0,0},{1,64},{2,128},{3,192},{4,256},{5,320},{6,384},{7,448},{8,16... | collective-permute-start | bytes 55304 | tf_op jit(solution)/shard_map/ppermute | solution.py:230
  89.4 2.9 %copy-start.8 = (f32[18,256]{1,0:T(8,128)}, f32[18,256]{1,0:T(8,128)S(1)}, u32[]{:S(2)}) copy-start(f32[18,256]{1,0:T(8,128)S(1)} %collective-permute-done.p_ref) | copy-start | bytes 55300
  92.3 0.8 copy-start.5
  120.8 17.4 %copy-start.6 = (f32[256,256]{1,0:T(8,128)S(1)}, f32[256,256]{1,0:T(8,128)}, u32[]{:S(2)}) copy-start(f32[256,256]{1,0:T(8,128)} %get-tuple-element.11.upper_ref) | copy-start | bytes 786436
  122.0 17.0 %all-to-all-start.4 = ((f32[4,288,256]{2,1,0:T(8,128)}), f32[4,288,256]{2,1,0:T(8,128)S(1)}, u32[]{:S(2)}, u32[]{:S(2)}) async-start(f32[4,288,256]{2,1,0:T(8,128)} %broadcast_in_dim.19), calls=%async_computation.4 | async-start | bytes 2359296 | tf_op jit(solution)/shard_map/all_to_all | solution.py:256
  126.3 45.6 %collective-permute-start.1 = (f32[18,256]{1,0:T(8,128)S(1)}, f32[18,256]{1,0:T(8,128)S(1)}, u32[]{:S(2)}, u32[]{:S(2)}) collective-permute-start(f32[18,256]{1,0:T(8,128)S(1)} %slice_bitcast_fusion), channel_id=1, source_target_pairs={{0,0},{64,1},{128,2},{192,3},{256,4},{320,5},{384,6},{448,7},{16,8... | collective-permute-start | bytes 55304 | tf_op jit(solution)/shard_map/ppermute | solution.py:257
  139.0 1.0 copy-start.3
  143.0 28.8 %all-to-all-start.5 = ((f32[16,16,256]{2,1,0:T(8,128)}), f32[16,16,256]{2,1,0:T(8,128)S(1)}, u32[]{:S(2)}, u32[]{:S(2)}) async-start(f32[16,16,256]{2,1,0:T(8,128)} %bitcast.25), calls=%async_computation.5 | async-start | bytes 524288 | tf_op jit(solution)/shard_map/all_to_all | solution.py:264
  171.8 19.4 %copy-start.2 = (f32[256,256]{1,0:T(8,128)S(1)}, f32[256,256]{1,0:T(8,128)}, u32[]{:S(2)}) copy-start(f32[256,256]{1,0:T(8,128)} %shard_map.30) | copy-start | bytes 786436
  191.1 1.1 copy-start.1
  191.2 1.4 copy-start.4
